TPU v7x, 256 devices: a whole 4x4x8 slice. The times are simulated.
256 devices in a mesh: blk: 32 (over y, z_hi, core), ij: 8 (over z_lo, x).
Axes of the slice: x: 4, y: 4, z: 8 (z_hi: 4, z_lo: 2; z = z_hi * 2 + z_lo), core: 2. Of those that a mesh axis runs over, the one named last changes fastest.
Arguments:
- density: float32 [32, 6, 256, 128], P('blk', None, 'ij'), may hold values from 0.8 to 1.2
- momentum: float32 [32, 3, 6, 256, 128], P('blk', None, None, 'ij'), may hold values from -2.5 to 2.5
- energy: float32 [32, 6, 256, 128], P('blk', None, 'ij'), may hold values from 2.5 to 4
- metrics: float32 [32, 4, 256, 128], P('blk', None, 'ij'), may hold values from -1 to 1
- volume: float32 [32, 256, 128], P('blk', 'ij'), may hold values from 0.5 to 2
- placed: int32 [32], replicated, may hold values from 0 to 31, each once
- neighbour: int32 [32, 2], replicated, may hold values from 0 to 31, as said below
- face: int32 [32, 2], replicated, may hold values from 0 to 1, as said below
- orient: int32 [32, 2], replicated, may hold values from 0 to 1, as said below
Outputs:
- next_density: float32 [32, 6, 256, 128], P('blk', None, 'ij')
- next_momentum: float32 [32, 3, 6, 256, 128], P('blk', None, None, 'ij')
- next_energy: float32 [32, 6, 256, 128], P('blk', None, 'ij')
Inputs may be any that keep to these rules, and one draw needn't show every extreme that they name: If face f of block b meets face g of block c with orientation o, then face g of c meets face f of b with orientation o; every block id appears as a neighbour. `face`: consistent with neighbour as stated there. `orient`: consistent with neighbour as stated there.
All inputs are finite; a program needn't handle non-finite values.
Results may differ from a plain program's by a relative error of at most 0.00002.
Values sent between devices are 32-bit elements; how exact they have to be, the bound alone decides.
A program may use at most 128 MiB of HBM per device.

v0:
```python
import jax
import jax.numpy as jnp
from jax import lax
from jax.sharding import PartitionSpec as P

pressure_factor = 0.4
viscosity = 0.05
conduction = 0.1
time_step = 0.03


def extended(value, sides, width):
    for axis, dim in sides:
        size, length = (lax.axis_size(axis), value.shape[dim])
        up = [(i, (i + 1) % size) for i in range(size - 1)]
        down = [(j, i) for i, j in up]
        last = lax.slice_in_dim(value, length - width, length, axis=dim)
        initial = lax.slice_in_dim(value, 0, width, axis=dim)
        before = lax.ppermute(last, axis, up)
        after = lax.ppermute(initial, axis, down)
        value = jnp.concatenate([before, value, after], axis=dim)
    return value


def slope_rows(f):
    return (
        f[..., 0:-4, 2:-2] - 8.0 * f[..., 1:-3, 2:-2] + 8.0 * f[..., 3:-1, 2:-2] - f[..., 4:, 2:-2]
    ) / 12.0


def slope_cols(f):
    return (
        f[..., 2:-2, 0:-4] - 8.0 * f[..., 2:-2, 1:-3] + 8.0 * f[..., 2:-2, 3:-1] - f[..., 2:-2, 4:]
    ) / 12.0


def slope_planes(f):
    return (
        jnp.roll(f, 2, -3)
        - 8.0 * jnp.roll(f, 1, -3)
        + 8.0 * jnp.roll(f, -1, -3)
        - jnp.roll(f, -2, -3)
    ) / 12.0


def curve_rows(f):
    return (
        -f[..., 0:-4, 2:-2]
        + 16.0 * f[..., 1:-3, 2:-2]
        - 30.0 * f[..., 2:-2, 2:-2]
        + 16.0 * f[..., 3:-1, 2:-2]
        - f[..., 4:, 2:-2]
    ) / 12.0


def curve_cols(f):
    return (
        -f[..., 2:-2, 0:-4]
        + 16.0 * f[..., 2:-2, 1:-3]
        - 30.0 * f[..., 2:-2, 2:-2]
        + 16.0 * f[..., 2:-2, 3:-1]
        - f[..., 2:-2, 4:]
    ) / 12.0


def curve_planes(f):
    return (
        -jnp.roll(f, 2, -3)
        + 16.0 * jnp.roll(f, 1, -3)
        - 30.0 * f
        + 16.0 * jnp.roll(f, -1, -3)
        - jnp.roll(f, -2, -3)
    ) / 12.0


def interior(f):
    return f[..., 2:-2, 2:-2]


def residual(ext):
    planes = ext.shape[1] - 1
    fields = ext[:, :planes]
    metric = ext[:, planes]
    dens = fields[0]
    moment = fields[1:4]
    energy_now = fields[4]
    velocity = moment / dens
    kinetic = 0.5 * jnp.sum(moment * velocity, axis=0)
    pressure = pressure_factor * (energy_now - kinetic)
    thermal = pressure / dens
    total_head = energy_now + pressure
    row_ax, row_ay, col_bx, col_by, cell_vol = (
        metric[0],
        metric[1],
        metric[2],
        metric[3],
        metric[4],
    )
    along_rows = row_ax * velocity[0] + row_ay * velocity[1]
    along_cols = col_bx * velocity[0] + col_by * velocity[1]
    flux_rows = cell_vol * jnp.stack(
        [
            dens * along_rows,
            moment[0] * along_rows + row_ax * pressure,
            moment[1] * along_rows + row_ay * pressure,
            moment[2] * along_rows,
            total_head * along_rows,
        ]
    )
    flux_cols = cell_vol * jnp.stack(
        [
            dens * along_cols,
            moment[0] * along_cols + col_bx * pressure,
            moment[1] * along_cols + col_by * pressure,
            moment[2] * along_cols,
            total_head * along_cols,
        ]
    )
    flux_planes = jnp.stack(
        [
            moment[2],
            moment[0] * velocity[2],
            moment[1] * velocity[2],
            moment[2] * velocity[2] + pressure,
            total_head * velocity[2],
        ]
    )
    inviscid = -(slope_rows(flux_rows) + slope_cols(flux_cols)) / interior(cell_vol) - slope_planes(
        interior(flux_planes)
    )
    row_weight = interior(row_ax * row_ax + row_ay * row_ay)
    col_weight = interior(col_bx * col_bx + col_by * col_by)

    def laplace(w):
        return row_weight * curve_rows(w) + col_weight * curve_cols(w) + curve_planes(interior(w))

    half_speed = kinetic / dens
    diffuse = jnp.stack(
        [
            jnp.zeros_like(inviscid[0]),
            viscosity * laplace(velocity[0]),
            viscosity * laplace(velocity[1]),
            viscosity * laplace(velocity[2]),
            viscosity * laplace(half_speed) + conduction * laplace(thermal),
        ]
    )
    return inviscid + diffuse


def wall_signs(planes):
    channel = jnp.arange(5)[:, None]
    plane_index = jnp.arange(planes)[None, :]
    flipped = (channel >= 1) & (channel <= 3) & (plane_index < planes - 1)
    return jnp.where(flipped, -1.0, 1.0)[:, :, None, None]


def ghost_factors(twisted, facing, planes):
    own_face = jnp.arange(2)[None, :]
    turn = jnp.where(twisted == 1, -1.0, 1.0)
    same = jnp.where(facing == own_face, -1.0, 1.0)
    channel = jnp.arange(5)[None, None, :]
    by_channel = jnp.where(
        channel < 2, turn[:, :, None], jnp.where(channel < 4, same[:, :, None], 1.0)
    )
    metric_plane = (jnp.arange(planes) == planes - 1)[None, None, None, :]
    return jnp.where(metric_plane, by_channel[:, :, :, None], 1.0)


def locate(placed):
    blocks = placed.shape[0]
    slots = jnp.arange(blocks, dtype=jnp.int32)
    return jnp.sum(jnp.where(placed[:, None] == slots[None, :], slots[:, None], 0), axis=0)


def pick_faces(target, facing, piece):
    piece_rows = piece.shape[0]
    slot_index = jnp.arange(piece_rows, dtype=jnp.int32)
    matched = target[:, :, None] == slot_index[None, None, :]
    chosen = jnp.where(
        facing[:, :, None, None, None, None, None] == 1,
        piece[None, None, :, 1],
        piece[None, None, :, 0],
    )
    return jnp.sum(jnp.where(matched[:, :, :, None, None, None, None], chosen, 0.0), axis=2)


def local(density, momentum, energy, metrics, volume, placed, neighbour, face, orient):
    local_count = density.shape[0]
    planes = density.shape[1] + 1
    fields = jnp.concatenate([density[:, None], momentum, energy[:, None]], axis=1)
    metric_plane = jnp.concatenate([metrics, volume[:, None]], axis=1)[:, :, None]
    split_count = lax.axis_size("ij")
    split_index = lax.axis_index("ij")
    group_index = lax.axis_index("blk")
    position = group_index * local_count + jnp.arange(local_count, dtype=jnp.int32)
    own_ids = placed[position]
    position_of = locate(placed)
    next_ids = neighbour[own_ids]
    facing = face[own_ids]
    twisted = orient[own_ids]
    partner = position_of[next_ids]
    factor = ghost_factors(twisted, facing, planes)[:, :, None, :, :, None]
    signs = wall_signs(planes)

    def extend(base):
        padded = extended(base, (("ij", 3),), 2)
        low_wall = base[:, :, :, 1::-1] * signs
        high_wall = base[:, :, :, -1:-3:-1]
        low_rows = jnp.where(split_index == 0, low_wall, padded[:, :, :, 0:2])
        high_rows = jnp.where(split_index == split_count - 1, high_wall, padded[:, :, :, -2:])
        rowed = jnp.concatenate([low_rows, base, high_rows], axis=3)
        strips = jnp.moveaxis(jnp.stack([base[..., 0:2], base[..., -1:-3:-1]], axis=1), -1, 2)
        source = partner // local_count * split_count + jnp.where(
            twisted == 1, split_count - 1 - split_index, split_index
        )
        target = source * local_count + partner % local_count
        ghosts = pick_faces(
            target, facing, lax.all_gather(strips, ("blk", "ij"), axis=0, tiled=True)
        )
        ghosts = jnp.where(twisted[:, :, None, None, None, None] == 1, ghosts[..., ::-1], ghosts)
        ghosts = jnp.moveaxis(ghosts * factor, 2, -1)
        left = jnp.pad(
            ghosts[:, 0][..., ::-1], ((0, 0), (0, 0), (0, 0), (2, 2), (0, 0)), constant_values=1.0
        )
        right = jnp.pad(ghosts[:, 1], ((0, 0), (0, 0), (0, 0), (2, 2), (0, 0)), constant_values=1.0)
        return jnp.concatenate([left, rowed, right], axis=-1)

    def tendency(state):
        return jax.vmap(residual)(extend(jnp.concatenate([state, metric_plane], axis=2)))

    section = fields + time_step * tendency(fields)
    result = 0.5 * fields + 0.5 * (section + time_step * tendency(section))
    return (result[:, 0], result[:, 1:4], result[:, 4])


def solution(mesh):
    return jax.shard_map(
        local,
        mesh=mesh,
        in_specs=(
            P("blk", None, "ij", None),
            P("blk", None, None, "ij", None),
            P("blk", None, "ij", None),
            P("blk", None, "ij", None),
            P("blk", "ij", None),
            P(),
            P(),
            P(),
            P(),
        ),
        out_specs=(
            P("blk", None, "ij", None),
            P("blk", None, None, "ij", None),
            P("blk", None, "ij", None),
        ),
        check_vma=False,
    )
```

profile of v0, /device:TPU:1, one launch (start us, length us, event | category | flops | bytes accessed | tf_op | source)
XLA Modules:
  0.0 1604.4 jit_solution(9384204103739592441)
XLA Ops:
  7.2 0.9 fusion.228
  8.1 1.1 fusion.49
  11.5 4.0 collective-permute-start
  15.5 1.3 collective-permute-start.1
  22.0 730.0 %all-gather.3.cloned.1.call-done = f32[256,2,2,5,7,32]{5,2,4,3,1,0:T(2,128)} async-done(((f32[1,2,2,5,7,32]{5,2,4,3,1,0:T(2,128)}), f32[256,2,2,5,7,32]{5,2,4,3,1,0:T(2,128)}) %all-gather.3.cloned.1.call-update) | async-done | bytes 4587536 | tf_op jit(solution)/shard_map/all_gather | solution.py:218
  752.0 18.2 %slice_bitcast_fusion.3 = (f32[256,2,5,7,32]{4,1,3,2,0:T(2,128)}, f32[256,2,5,7,32]{4,1,3,2,0:T(2,128)}) fusion(f32[256,2,2,5,7,32]{5,2,4,3,1,0:T(2,128)} %all-gather.3.cloned.1.call-done), kind=kLoop, calls=%fused_computation.4 | loop fusion | bytes 9175040 | tf_op jit(solution)/shard_map/jit(_where)/broadcast_in_dim | solution.py:179
  770.2 9.6 copy.248
  779.8 11.1 copy.249
  790.9 2.6 select_reduce_fusion.1
  795.1 0.8 fusion.281
  800.1 0.9 fusion.170
  801.1 0.9 fusion.157
  802.0 0.9 fusion.144
  802.9 1.1 fusion.120
  804.0 2.1 multiply_add_fusion
  809.0 1.3 collective-permute-start.3
  810.4 4.2 collective-permute-start.2
  815.5 729.3 %all-gather.5.cloned.1.call-done = f32[256,2,2,5,7,32]{5,2,4,3,1,0:T(2,128)} async-done(((f32[1,2,2,5,7,32]{5,2,4,3,1,0:T(2,128)}), f32[256,2,2,5,7,32]{5,2,4,3,1,0:T(2,128)}) %all-gather.5.cloned.1.call-update) | async-done | bytes 4587536 | tf_op jit(solution)/shard_map/all_gather | solution.py:218
  1544.8 18.2 %slice_bitcast_fusion.1 = (f32[256,2,5,7,32]{4,1,3,2,0:T(2,128)}, f32[256,2,5,7,32]{4,1,3,2,0:T(2,128)}) fusion(f32[256,2,2,5,7,32]{5,2,4,3,1,0:T(2,128)} %all-gather.5.cloned.1.call-done), kind=kLoop, calls=%fused_computation.2 | loop fusion | bytes 9175040 | tf_op jit(solution)/shard_map/jit(_where)/broadcast_in_dim | solution.py:179
  1563.1 9.6 copy.281
  1572.6 11.1 copy.282
  1583.8 2.6 select_reduce_fusion
  1593.0 0.9 copy-done.5
  1595.2 1.0 add_multiply_fusion
  (183 shorter events, 24.1 us)
Async XLA Ops:
  7.2 12.2 copy-start
  7.2 744.8 %all-gather.3.cloned.1.call-start = ((), (), s32[]{:S(2)}) async-start(), calls=%async_computation | async-start | bytes 18421760 | tf_op jit(solution)/shard_map/all_gather | solution.py:218
  10.4 6.4 copy-start.8
  10.4 9.2 copy-start.6
  10.6 9.8 copy-start.7
  11.4 1533.5 %all-gather.5.cloned.1.call-start = ((), (), s32[]{:S(2)}) async-start(), calls=%async_computation.1 | async-start | bytes 18421760 | tf_op jit(solution)/shard_map/all_gather | solution.py:218
  11.5 10.4 collective-permute-start
  15.5 6.4 collective-permute-start.1
  802.9 1.1 copy-start.2
  802.9 1.1 copy-start.3
  802.9 1.1 copy-start.4
  809.0 5.7 collective-permute-start.3
  810.4 5.0 collective-permute-start.2
  1592.8 1.0 copy-start.5
  1595.2 2.4 copy-start.1
Sparse Core Ops, SparseCore 0:
  11.5 740.4 all-gather.2
  808.4 736.3 all-gather.4
where the time goes:
time: 1610 us; the launch traced here: 1600 us
  waiting for transfers between devices  1460 us (91%)
  local copies, waits for them, and re-layouts  92.8 us (6%)
  other arithmetic  24 us (1%)
  between operations  16.8 us (1%)
    all_gather x2, waiting for transfers between devices, extend(): lax.all_gather(strips, ('blk', 'ij'), axis=0, tiled=True)  1460 us
    broadcast_in_dim x6, local copies, waits for them, and re-layouts, pick_faces(): jnp.where(facing[:, :, None, None, None, None, None] == 1, piece[None, No...  77.9 us
  transfers between devices with their start and end apart: 6, of which 3 were waited for; matrix products, arithmetic and copies ran while one was open for 0% of the time, Pallas kernels for 0%

commit v1 on v0

v1 whole, which is shorter than its diff:
```python
import functools

import jax
import jax.numpy as jnp
from jax import lax
from jax.experimental import pallas as pl
from jax.experimental.pallas import tpu as pltpu
from jax.sharding import PartitionSpec as P

MESH = pl.DeviceIdType.MESH
pressure_factor = 0.4
viscosity = 0.05
conduction = 0.1
time_step = 0.03
ROWS, COLS, PLANES, CHUNK = 32, 128, 6, 8
Y, Z, CORES, IJ, BLOCKS = 4, 4, 2, 8, 32
STRIP = (ROWS, COLS)


def lanes(shape):
    return lax.broadcasted_iota(jnp.int32, shape, len(shape) - 1)


def shift_lanes(x, by):
    by = by % COLS
    return x if by == 0 else pltpu.roll(x, by, x.ndim - 1)


def primitives(rho, m1, m2, m3, energy, dt):
    inv = 1.0 / rho
    u1, u2, u3 = m1 * inv, m2 * inv, m3 * inv
    kinetic = 0.5 * (m1 * u1 + m2 * u2 + m3 * u3)
    p = pressure_factor * (energy - kinetic)
    head = energy + p
    soft = dt * viscosity / 12.0
    warm = dt * conduction / 12.0
    curved = (soft * u1, soft * u2, soft * u3, inv * (soft * kinetic + warm * p))
    return u1, u2, u3, p, head, curved


def flux(rho, m1, m2, m3, prim, gx, gy):
    u1, u2, u3, p, head, _ = prim
    speed = gx * u1 + gy * u2
    return (rho * speed, m1 * speed + gx * p, m2 * speed + gy * p, m3 * speed, head * speed)


def slope(b2, b1, a1, a2):
    return 8.0 * (a1 - b1) - (a2 - b2)


def curve(b2, b1, a1, a2):
    return 16.0 * (a1 + b1) - (a2 + b2)


def plane_shift(f, by):
    by = by % PLANES
    return jnp.concatenate([f[by:], f[:by]], axis=0)


def chunk_metrics(met, vol, c, dt):
    rows = slice(c * CHUNK, (c + 1) * CHUNK)
    ax, ay, bx, by = (met[0, n, rows, :] for n in range(4))
    v = vol[0, rows, :]
    return (v * ax, v * ay, v * bx, v * by, (dt / 12.0) / v, ax * ax + ay * ay, bx * bx + by * by)


def before_ghosts(get, met, vol, fi, wi, part, dt):
    for c in range(ROWS // CHUNK):
        rows = slice(c * CHUNK, (c + 1) * CHUNK)
        gax, gay, gbx, gby, iv, rw, cw = chunk_metrics(met, vol, c, dt)
        center = -30.0 * (rw + cw + 1.0)
        rho, m1, m2, m3, energy = (get(ch, rows) for ch in range(5))
        prim = primitives(rho, m1, m2, m3, energy, dt)
        u1, u2, u3, p, head, curved = prim
        inner = slice(CHUNK + c * CHUNK, 2 * CHUNK + c * CHUNK)
        for ch, f in enumerate(flux(rho, m1, m2, m3, prim, gax, gay)):
            fi[ch, :, inner, :] = f
        for n, w in enumerate(curved):
            wi[n, :, inner, :] = w
        fj = flux(rho, m1, m2, m3, prim, gbx, gby)
        fk = (m3, m1 * u3, m2 * u3, m3 * u3 + p, head * u3)
        for ch in range(5):
            f, g = fj[ch], fk[ch]
            dj = slope(*(shift_lanes(f, by) for by in (2, 1, -1, -2)))
            dk = slope(*(plane_shift(g, by) for by in (-2, -1, 1, 2)))
            total = -(dj * iv) - (dt / 12.0) * dk
            if ch > 0:
                w = curved[ch - 1]
                sj = curve(*(shift_lanes(w, by) for by in (2, 1, -1, -2)))
                sk = curve(*(plane_shift(w, by) for by in (-2, -1, 1, 2)))
                total = total + cw * sj + sk + center * w
            part[ch, :, rows, :] = total


def halo_rows(get_halo, fi, wi, dt):
    for n in range(4):
        at = (CHUNK - 2, CHUNK - 1, CHUNK + ROWS, CHUNK + ROWS + 1)[n]
        block = get_halo(n)
        rho, m1, m2, m3, energy = (block[6 * ch : 6 * ch + 6, :] for ch in range(5))
        gax, gay = block[30:31, :], block[31:32, :]
        prim = primitives(rho, m1, m2, m3, energy, dt)
        for ch, f in enumerate(flux(rho, m1, m2, m3, prim, gax, gay)):
            for k in range(PLANES):
                fi[ch, k, at : at + 1, :] = f[k : k + 1, :]
        for m, w in enumerate(prim[5]):
            for k in range(PLANES):
                wi[m, k, at : at + 1, :] = w[k : k + 1, :]


def spread(x):
    x = jnp.where(lanes(x.shape) < 4, x, 0.0)
    pair = x + shift_lanes(x, 4)
    return pair + shift_lanes(pair, 8) + shift_lanes(pair, 16)


def edge_values(strip, dt):
    rho, m1, m2, m3, energy = (shift_lanes(strip, -24 * ch) for ch in range(5))
    gbx, gby = spread(shift_lanes(strip, -120)), spread(shift_lanes(strip, -124))
    prim = primitives(rho, m1, m2, m3, energy, dt)
    return flux(rho, m1, m2, m3, prim, gbx, gby) + prim[5]


def edge_terms(own, ghost, edge, dt):
    upper = (lanes(STRIP) & 3) >= 2
    mine, theirs = edge_values(own, dt), edge_values(ghost, dt)
    for n in range(9):
        h = theirs[n] - mine[n]
        high, low = jnp.where(upper, h, 0.0), jnp.where(upper, 0.0, h)
        if n < 5:
            left = 8.0 * shift_lanes(high, -1) - shift_lanes(high, -2)
            right = shift_lanes(low, 2) - 8.0 * shift_lanes(low, 1)
        else:
            left = 16.0 * shift_lanes(high, -1) - shift_lanes(high, -2)
            right = 16.0 * shift_lanes(low, 1) - shift_lanes(low, 2)
        edge[n] = jnp.where(upper, right, left)


def after_ghosts(put, met, vol, fi, wi, part, edge, dt):
    at = lanes((CHUNK, COLS))
    border = (at < 2) | (at >= COLS - 2)
    for c in range(ROWS // CHUNK):
        rows = slice(c * CHUNK, (c + 1) * CHUNK)
        gax, gay, gbx, gby, iv, rw, cw = chunk_metrics(met, vol, c, dt)
        base = CHUNK + c * CHUNK
        for ch in range(5):
            di = slope(*(fi[ch, :, base + d : base + d + CHUNK, :] for d in (-2, -1, 1, 2)))
            total = part[ch, :, rows, :] - di * iv
            if ch > 0:
                si = curve(*(wi[ch - 1, :, base + d : base + d + CHUNK, :] for d in (-2, -1, 1, 2)))
                total = total + rw * si
            terms = []
            for k in range(PLANES):
                term = -(shift_lanes(edge[ch, rows, :], -4 * k - 2) * iv)
                if ch > 0:
                    term = term + cw * shift_lanes(edge[4 + ch, rows, :], -4 * k - 2)
                terms.append(jnp.where(border, term, 0.0))
            put(ch, rows, total + jnp.stack(terms, axis=0))


def pack(get, met, vol, strips, rows_out):
    at = lanes(STRIP) >> 2
    every = slice(0, ROWS)
    v = vol[0]
    acc = jnp.zeros(STRIP, jnp.float32)
    for q in range(32):
        x = get(q // 6, every, q % 6) if q < 30 else v * met[0, q - 28]
        acc = jnp.where(at == q, shift_lanes(x, 2 + 4 * q), acc)
    strips[0] = acc
    for r in range(ROWS):
        strips[1, ROWS - 1 - r : ROWS - r, :] = strips[0, r : r + 1, :]
    for n, r in enumerate((0, 1, ROWS - 2, ROWS - 1)):
        row = slice(r, r + 1)
        for q in range(32):
            x = get(q // 6, row, q % 6) if q < 30 else vol[0, row, :] * met[0, q - 30, row, :]
            rows_out[n, q : q + 1, :] = x


def peers_first(y, z, c, s):
    out = []
    for dz in range(Z):
        for m in range(2):
            blk = (y * Z + lax.rem(z + dz, Z)) * CORES + c
            out.append({"blk": blk, "ij": (IJ - 1 - s) if m else s})
    return out


def peers_second(y, z, c, s):
    out = []
    for dy in range(Y):
        for dc in range(2):
            blk = (lax.rem(y + dy, Y) * Z + z) * CORES + (1 - c if dc else c)
            out.append({"blk": blk, "ij": s})
    return out


def routes(placed, neighbour, face, orient, targets):
    ids = [placed[t["blk"]] for t in targets]
    wanted = [(b, f) for b in ids for f in range(2)]
    nids = [neighbour[b, f] for b, f in wanted]

    def find(p, found):
        held = placed[p]
        return tuple(jnp.where(n == held, p, a) for n, a in zip(nids, found))

    found = lax.fori_loop(0, BLOCKS, find, tuple(jnp.int32(0) for _ in nids))
    return [(q, face[b, f], orient[b, f]) for q, (b, f) in zip(found, wanted)]


def body(
    placed, neighbour, face, orient, dens, mom, ener, met, vol,
    out_d, out_m, out_e,
    sec, fi, wi, part, edge, strips, rows_out, rows_in, got, both, picked, got2a, got2b,
    send1, recv1, send2, recv2, send_r, recv_r,
):
    b, s = lax.axis_index("blk"), lax.axis_index("ij")
    c = lax.rem(b, CORES)
    z = lax.rem(b // CORES, Z)
    y = b // (CORES * Z)
    first, second = peers_first(y, z, c, s), peers_second(y, z, c, s)
    below = {"blk": b, "ij": lax.rem(s + IJ - 1, IJ)}
    above = {"blk": b, "ij": lax.rem(s + 1, IJ)}
    everyone = first[1:] + second[1:] + [below, above]
    barrier = pltpu.get_barrier_semaphore()
    for peer in everyone:
        pl.semaphore_signal(barrier, inc=1, device_id=peer, device_id_type=MESH)

    def get_input(ch, rows, plane=slice(None)):
        if ch == 0:
            return dens[0, plane, rows, :]
        if ch == 4:
            return ener[0, plane, rows, :]
        return mom[0, ch - 1, plane, rows, :]

    def get_section(ch, rows, plane=slice(None)):
        return sec[ch, plane, rows, :]

    def put_section(ch, rows, change):
        sec[ch, :, rows, :] = get_input(ch, rows) + change

    def put_result(ch, rows, change):
        value = 0.5 * (get_input(ch, rows) + get_section(ch, rows)) + change
        if ch == 0:
            out_d[0, :, rows, :] = value
        elif ch == 4:
            out_e[0, :, rows, :] = value
        else:
            out_m[0, ch - 1, :, rows, :] = value

    wall_sign = jnp.where(
        (lax.broadcasted_iota(jnp.int32, STRIP, 0) >= 6)
        & (lax.broadcasted_iota(jnp.int32, STRIP, 0) < 24),
        -1.0,
        1.0,
    )
    group = lanes(STRIP) & 3
    metric_sign = jnp.where(lanes(STRIP) >= 120, -1.0, 1.0)
    table = []

    for turn, (get, put, dt) in enumerate(
        ((get_input, put_section, time_step), (get_section, put_result, 0.5 * time_step))
    ):
        got2 = (got2a, got2b)[turn]
        pack(get, met, vol, strips.at[turn], rows_out.at[turn])
        if turn == 0:
            pl.semaphore_wait(barrier, len(everyone))
        hop1 = [
            pltpu.make_async_remote_copy(
                src_ref=strips.at[turn, k % 2],
                dst_ref=got.at[turn, k],
                send_sem=send1.at[turn, k],
                recv_sem=recv1.at[turn, k],
                device_id=first[k],
                device_id_type=MESH,
            )
            for k in range(1, 8)
        ]
        for copy in hop1:
            copy.start()
        slide = [
            pltpu.make_async_remote_copy(
                src_ref=rows_out.at[turn, pl.ds(2 * side, 2)],
                dst_ref=rows_in.at[turn, pl.ds(2 - 2 * side, 2)],
                send_sem=send_r.at[turn, side],
                recv_sem=recv_r.at[turn, side],
                device_id=(below, above)[side],
                device_id_type=MESH,
            )
            for side in range(2)
        ]
        for copy in slide:
            copy.start()
        if turn == 0:
            table.extend(routes(placed, neighbour, face, orient, second))
        before_ghosts(get, met, vol, fi, wi, part, dt)
        for k in range(8):
            if k > 0:
                hop1[k - 1].wait_recv()
                x = got[turn, k]
            else:
                x = strips[turn, 0]
            both[turn, k] = x
            flipped = jnp.where(group == 0, shift_lanes(x, -3), shift_lanes(x, -1))
            flipped = jnp.where(group == 2, shift_lanes(x, 1), flipped)
            flipped = jnp.where(group == 3, shift_lanes(x, 3), flipped)
            both[turn, 8 + k] = flipped * metric_sign
        hop2 = []
        for k in range(8):
            parts = []
            for f in range(2):
                q, g, o = table[2 * k + f]
                dz = lax.rem(z - lax.rem(q // CORES, Z) + Z, Z)
                parts.append(both[turn, jnp.where(g == f, 8, 0) + 2 * dz + o])
            message = jnp.where(group < 2, parts[0], parts[1])
            if k == 0:
                got2[0] = message
            else:
                picked[turn, k] = message
                copy = pltpu.make_async_remote_copy(
                    src_ref=picked.at[turn, k],
                    dst_ref=got2.at[k],
                    send_sem=send2.at[turn, k],
                    recv_sem=recv2.at[turn, k],
                    device_id=second[k],
                    device_id_type=MESH,
                )
                copy.start()
                hop2.append(copy)
        for copy in slide:
            copy.wait_recv()

        def get_halo(n):
            own = rows_out[turn, (1, 0, 3, 2)[n]]
            if n < 2:
                return jnp.where(s == 0, wall_sign * own, rows_in[turn, n])
            return jnp.where(s == IJ - 1, own, rows_in[turn, n])

        halo_rows(get_halo, fi, wi, dt)
        for copy in hop2:
            copy.wait_recv()
        sides = []
        for f in range(2):
            q, g, o = table[f]
            dy = lax.rem(y - q // (CORES * Z) + Y, Y)
            dc = jnp.where(lax.rem(q, CORES) == c, 0, 1)
            sides.append(got2[2 * dy + dc])
        ghost = jnp.where(group < 2, sides[0], sides[1])
        edge_terms(strips[turn, 0], ghost, edge, dt)
        after_ghosts(put, met, vol, fi, wi, part, edge, dt)
        for copy in hop1 + slide + hop2:
            copy.wait_send()


def local(density, momentum, energy, metrics, volume, placed, neighbour, face, orient):
    smem = pl.BlockSpec(memory_space=pltpu.SMEM)
    vmem = pl.BlockSpec(memory_space=pltpu.VMEM)
    f32 = jnp.float32
    dma = pltpu.SemaphoreType.DMA
    padded = ROWS + 2 * CHUNK
    return pl.pallas_call(
        body,
        out_shape=tuple(jax.ShapeDtypeStruct(x.shape, f32) for x in (density, momentum, energy)),
        in_specs=[smem] * 4 + [vmem] * 5,
        out_specs=(vmem, vmem, vmem),
        scratch_shapes=[
            pltpu.VMEM((5, PLANES, ROWS, COLS), f32),
            pltpu.VMEM((5, PLANES, padded, COLS), f32),
            pltpu.VMEM((4, PLANES, padded, COLS), f32),
            pltpu.VMEM((5, PLANES, ROWS, COLS), f32),
            pltpu.VMEM((9, ROWS, COLS), f32),
            pltpu.VMEM((2, 2, ROWS, COLS), f32),
            pltpu.VMEM((2, 4, ROWS, COLS), f32),
            pltpu.VMEM((2, 4, ROWS, COLS), f32),
            pltpu.VMEM((2, 8, ROWS, COLS), f32),
            pltpu.VMEM((2, 16, ROWS, COLS), f32),
            pltpu.VMEM((2, 8, ROWS, COLS), f32),
            pltpu.VMEM((8, ROWS, COLS), f32),
            pltpu.VMEM((8, ROWS, COLS), f32),
            dma((2, 8)), dma((2, 8)), dma((2, 8)), dma((2, 8)), dma((2, 2)), dma((2, 2)),
        ],
        compiler_params=pltpu.CompilerParams(
            collective_id=0, has_side_effects=True, vmem_limit_bytes=32 << 20
        ),
    )(placed, neighbour, face, orient, density, momentum, energy, metrics, volume)


def solution(mesh):
    return jax.shard_map(
        local,
        mesh=mesh,
        in_specs=(
            P("blk", None, "ij", None),
            P("blk", None, None, "ij", None),
            P("blk", None, "ij", None),
            P("blk", None, "ij", None),
            P("blk", "ij", None),
            P(),
            P(),
            P(),
            P(),
        ),
        out_specs=(
            P("blk", None, "ij", None),
            P("blk", None, None, "ij", None),
            P("blk", None, "ij", None),
        ),
        check_vma=False,
    )
```

time: 1610 us -> 45.3 us (0.03)
  waiting for transfers between devices: 1460 us -> 0 us
  local copies, waits for them, and re-layouts: 92.8 us -> 7.68 us
  Pallas kernels: 0 us -> 36.6 us
  other arithmetic: 24 us -> 0 us
  between operations: 16.8 us -> 0.66 us
    all_gather x2 -> x0, waiting for transfers between devices: 1460 us -> none  [extend(): lax.all_gather(strips, ('blk', 'ij'), axis=0, tiled=True)]
    broadcast_in_dim x6 -> x0, local copies, waits for them, and re-layouts: 77.9 us -> none  [pick_faces(): jnp.where(facing[:, :, None, None, None, None, None] == 1, piece[None, No...]
    pallas_call x0 -> x1, Pallas kernels: none -> 36.6 us  [local(): pl.pallas_call(body, out_shape=tuple((jax.ShapeDtypeStruct(x.shape, f32)...]
  transfers between devices with their start and end apart: 6 -> 0, of which waited for: 3 -> 0; matrix products, arithmetic and copies ran while one was open for 0% -> 0% of each run, Pallas kernels for 0% -> 0%
where the time goes in v1:
time: 45.3 us; the launch traced here: 45 us
  Pallas kernels  36.6 us (81%)
  local copies, waits for them, and re-layouts  7.68 us (17%)
  between operations  0.66 us (1%)
    pallas_call x1, Pallas kernels, local(): pl.pallas_call(body, out_shape=tuple((jax.ShapeDtypeStruct(x.shape, f32)...  36.6 us
    unnamed x22, local copies, waits for them, and re-layouts  7.68 us

profile of v1, /device:TPU:1, one launch (start us, length us, event | category | flops | bytes accessed | tf_op | source)
XLA Modules:
  0.0 45.0 jit_solution(13572667221200257828)
XLA Ops:
  0.6 0.0 copy-start.6
  0.6 0.8 %copy.12.neighbour = s32[32,2]{1,0:T(8,128)S(1)} copy(s32[32,2]{0,1:T(2,128)} %param.15) | data formatting | bytes 512 | tf_op args[6]
  1.4 0.0 copy-done.6
  1.4 0.0 copy-start.7
  1.4 0.0 copy-start.4
  1.4 0.1 copy.13.face
  1.5 0.6 %copy-done.7 = s32[32,2]{0,1:T(2,128)S(1)} copy-done((s32[32,2]{0,1:T(2,128)S(1)}, s32[32,2]{0,1:T(2,128)}, u32[]{:S(2)}) %copy-start.7) | copy-done | bytes 280
  2.1 0.0 copy-start.5
  2.1 0.1 copy.14.orient
  2.2 0.0 copy-done.4
  2.2 0.6 %copy-done.5 = s32[32]{0:T(128)S(1)} copy-done((s32[32]{0:T(128)S(1)}, s32[32]{0:T(128)}, u32[]{:S(2)}) %copy-start.5) | copy-done | bytes 152
  2.7 0.0 copy-start
  2.7 1.0 %copy-done = f32[1,3,6,32,128]{4,3,2,1,0:T(8,128)S(1)} copy-done((f32[1,3,6,32,128]{4,3,2,1,0:T(8,128)S(1)}, f32[1,3,6,32,128]{4,3,2,1,0:T(8,128)}, u32[]{:S(2)}) %copy-start) | copy-done | bytes 294936
  3.7 0.0 copy-start.1
  3.7 0.9 %copy-done.1 = f32[1,6,32,128]{3,2,1,0:T(8,128)S(1)} copy-done((f32[1,6,32,128]{3,2,1,0:T(8,128)S(1)}, f32[1,6,32,128]{3,2,1,0:T(8,128)}, u32[]{:S(2)}) %copy-start.1) | copy-done | bytes 98328
  4.6 0.0 copy-start.2
  4.6 0.9 %copy-done.2 = f32[1,6,32,128]{3,2,1,0:T(8,128)S(1)} copy-done((f32[1,6,32,128]{3,2,1,0:T(8,128)S(1)}, f32[1,6,32,128]{3,2,1,0:T(8,128)}, u32[]{:S(2)}) %copy-start.2) | copy-done | bytes 98328
  5.5 0.0 copy-start.3
  5.5 0.8 %copy-done.3 = f32[1,4,32,128]{3,2,1,0:T(8,128)S(1)} copy-done((f32[1,4,32,128]{3,2,1,0:T(8,128)S(1)}, f32[1,4,32,128]{3,2,1,0:T(8,128)}, u32[]{:S(2)}) %copy-start.3) | copy-done | bytes 65560
  6.3 36.6 %shard_map.112 = (f32[1,6,32,128]{3,2,1,0:T(8,128)S(1)}, f32[1,3,6,32,128]{4,3,2,1,0:T(8,128)S(1)}, f32[1,6,32,128]{3,2,1,0:T(8,128)S(1)}) custom-call(s32[32]{0:T(128)S(1)} %copy-done.5, s32[32,2]{1,0:T(8,128)S(1)} %copy.12.neighbour, s32[32,2]{1,0:T(8,128)S(1)} %copy.13.face, s32[32,2]{1,0:T(8,128)S(1)} %copy.14.orient, f32[1,6,32,128]{3,2,1,0:T(8,128)S(1)} %copy-done.1, ...), custom_call_target="tpu_custom_call" | custom-call | tf_op jit(solution)/shard_map/pallas_call | solution.py:359
  43.0 0.6 %copy.18 = f32[1,6,32,128]{3,2,1,0:T(8,128)} copy(f32[1,6,32,128]{3,2,1,0:T(8,128)S(1)} %get-tuple-element.6) | data formatting | bytes 196608
  43.6 0.7 %copy.19 = f32[1,3,6,32,128]{4,3,2,1,0:T(8,128)} copy(f32[1,3,6,32,128]{4,3,2,1,0:T(8,128)S(1)} %get-tuple-element.7) | data formatting | bytes 589824
  44.3 0.6 %copy.20 = f32[1,6,32,128]{3,2,1,0:T(8,128)} copy(f32[1,6,32,128]{3,2,1,0:T(8,128)S(1)} %get-tuple-element.8) | data formatting | bytes 196608
Async XLA Ops:
  0.6 0.8 %copy-start.6 = (s32[32,2]{0,1:T(2,128)S(1)}, s32[32,2]{0,1:T(2,128)}, u32[]{:S(2)}) copy-start(s32[32,2]{0,1:T(2,128)} %param.16) | copy-start | bytes 772
  1.4 0.7 %copy-start.7 = (s32[32,2]{0,1:T(2,128)S(1)}, s32[32,2]{0,1:T(2,128)}, u32[]{:S(2)}) copy-start(s32[32,2]{0,1:T(2,128)} %param.17) | copy-start | bytes 772
  1.4 0.8 %copy-start.4 = (f32[1,32,128]{2,1,0:T(8,128)S(1)}, f32[1,32,128]{2,1,0:T(8,128)}, u32[]{:S(2)}) copy-start(f32[1,32,128]{2,1,0:T(8,128)} %vol.1) | copy-start | bytes 49156
  2.1 0.7 %copy-start.5 = (s32[32]{0:T(128)S(1)}, s32[32]{0:T(128)}, u32[]{:S(2)}) copy-start(s32[32]{0:T(128)} %placed.1) | copy-start | bytes 388
  2.7 1.0 %copy-start = (f32[1,3,6,32,128]{4,3,2,1,0:T(8,128)S(1)}, f32[1,3,6,32,128]{4,3,2,1,0:T(8,128)}, u32[]{:S(2)}) copy-start(f32[1,3,6,32,128]{4,3,2,1,0:T(8,128)} %mom.1) | copy-start | bytes 884740
  3.7 0.9 %copy-start.1 = (f32[1,6,32,128]{3,2,1,0:T(8,128)S(1)}, f32[1,6,32,128]{3,2,1,0:T(8,128)}, u32[]{:S(2)}) copy-start(f32[1,6,32,128]{3,2,1,0:T(8,128)} %dens.1) | copy-start | bytes 294916
  4.6 0.9 %copy-start.2 = (f32[1,6,32,128]{3,2,1,0:T(8,128)S(1)}, f32[1,6,32,128]{3,2,1,0:T(8,128)}, u32[]{:S(2)}) copy-start(f32[1,6,32,128]{3,2,1,0:T(8,128)} %ener.1) | copy-start | bytes 294916
  5.5 0.8 %copy-start.3 = (f32[1,4,32,128]{3,2,1,0:T(8,128)S(1)}, f32[1,4,32,128]{3,2,1,0:T(8,128)}, u32[]{:S(2)}) copy-start(f32[1,4,32,128]{3,2,1,0:T(8,128)} %met.1) | copy-start | bytes 196612

commit v2 on v1

--- a/solution.py
+++ b/solution.py
@@ -196,22 +196,34 @@
 def routes(placed, neighbour, face, orient, targets):
     ids = [placed[t["blk"]] for t in targets]
     wanted = [(b, f) for b in ids for f in range(2)]
-    nids = [neighbour[b, f] for b, f in wanted]
+    nids = [neighbour[f, b] for b, f in wanted]
 
     def find(p, found):
         held = placed[p]
         return tuple(jnp.where(n == held, p, a) for n, a in zip(nids, found))
 
     found = lax.fori_loop(0, BLOCKS, find, tuple(jnp.int32(0) for _ in nids))
-    return [(q, face[b, f], orient[b, f]) for q, (b, f) in zip(found, wanted)]
+    return [(q, face[f, b], orient[f, b]) for q, (b, f) in zip(found, wanted)]
 
 
 def body(
-    placed, neighbour, face, orient, dens, mom, ener, met, vol,
+    placed_hbm, neighbour_hbm, face_hbm, orient_hbm, dens_hbm, mom_hbm, ener_hbm, met_hbm, vol_hbm,
     out_d, out_m, out_e,
+    placed, neighbour, face, orient, dens, mom, ener, met, vol, load,
     sec, fi, wi, part, edge, strips, rows_out, rows_in, got, both, picked, got2a, got2b,
     send1, recv1, send2, recv2, send_r, recv_r,
 ):
+    fetch = [
+        pltpu.make_async_copy(src, dst, load.at[n])
+        for n, (src, dst) in enumerate(
+            (
+                (mom_hbm, mom), (dens_hbm, dens), (ener_hbm, ener), (met_hbm, met), (vol_hbm, vol),
+                (placed_hbm, placed), (neighbour_hbm, neighbour), (face_hbm, face), (orient_hbm, orient),
+            )
+        )
+    ]
+    for copy in fetch:
+        copy.start()
     b, s = lax.axis_index("blk"), lax.axis_index("ij")
     c = lax.rem(b, CORES)
     z = lax.rem(b // CORES, Z)
@@ -223,6 +235,9 @@
     barrier = pltpu.get_barrier_semaphore()
     for peer in everyone:
         pl.semaphore_signal(barrier, inc=1, device_id=peer, device_id_type=MESH)
+
+    for copy in fetch:
+        copy.wait()
 
     def get_input(ch, rows, plane=slice(None)):
         if ch == 0:
@@ -350,37 +365,64 @@
             copy.wait_send()
 
 
+def hand_over(d, m, e, out_d, out_m, out_e, sems):
+    copies = [
+        pltpu.make_async_copy(src, dst, sems.at[n])
+        for n, (src, dst) in enumerate(((m, out_m), (d, out_d), (e, out_e)))
+    ]
+    for copy in copies:
+        copy.start()
+    for copy in copies:
+        copy.wait()
+
+
 def local(density, momentum, energy, metrics, volume, placed, neighbour, face, orient):
-    smem = pl.BlockSpec(memory_space=pltpu.SMEM)
-    vmem = pl.BlockSpec(memory_space=pltpu.VMEM)
-    f32 = jnp.float32
+    smem, vmem, i32, f32 = pltpu.SMEM, pltpu.VMEM, jnp.int32, jnp.float32
+    anywhere = pl.BlockSpec(memory_space=pltpu.HBM)
+    inside = pl.BlockSpec(memory_space=pltpu.VMEM)
     dma = pltpu.SemaphoreType.DMA
     padded = ROWS + 2 * CHUNK
-    return pl.pallas_call(
+    shapes = tuple(jax.ShapeDtypeStruct(x.shape, f32) for x in (density, momentum, energy))
+    results = pl.pallas_call(
         body,
-        out_shape=tuple(jax.ShapeDtypeStruct(x.shape, f32) for x in (density, momentum, energy)),
-        in_specs=[smem] * 4 + [vmem] * 5,
-        out_specs=(vmem, vmem, vmem),
+        out_shape=shapes,
+        in_specs=[anywhere] * 9,
+        out_specs=(inside,) * 3,
         scratch_shapes=[
-            pltpu.VMEM((5, PLANES, ROWS, COLS), f32),
-            pltpu.VMEM((5, PLANES, padded, COLS), f32),
-            pltpu.VMEM((4, PLANES, padded, COLS), f32),
-            pltpu.VMEM((5, PLANES, ROWS, COLS), f32),
-            pltpu.VMEM((9, ROWS, COLS), f32),
-            pltpu.VMEM((2, 2, ROWS, COLS), f32),
-            pltpu.VMEM((2, 4, ROWS, COLS), f32),
-            pltpu.VMEM((2, 4, ROWS, COLS), f32),
-            pltpu.VMEM((2, 8, ROWS, COLS), f32),
-            pltpu.VMEM((2, 16, ROWS, COLS), f32),
-            pltpu.VMEM((2, 8, ROWS, COLS), f32),
-            pltpu.VMEM((8, ROWS, COLS), f32),
-            pltpu.VMEM((8, ROWS, COLS), f32),
+            smem((BLOCKS,), i32), smem((2, BLOCKS), i32), smem((2, BLOCKS), i32), smem((2, BLOCKS), i32),
+            vmem(density.shape, f32), vmem(momentum.shape, f32), vmem(energy.shape, f32),
+            vmem(metrics.shape, f32), vmem(volume.shape, f32), dma((9,)),
+            vmem((5, PLANES, ROWS, COLS), f32),
+            vmem((5, PLANES, padded, COLS), f32),
+            vmem((4, PLANES, padded, COLS), f32),
+            vmem((5, PLANES, ROWS, COLS), f32),
+            vmem((9, ROWS, COLS), f32),
+            vmem((2, 2, ROWS, COLS), f32),
+            vmem((2, 4, ROWS, COLS), f32),
+            vmem((2, 4, ROWS, COLS), f32),
+            vmem((2, 8, ROWS, COLS), f32),
+            vmem((2, 16, ROWS, COLS), f32),
+            vmem((2, 8, ROWS, COLS), f32),
+            vmem((8, ROWS, COLS), f32),
+            vmem((8, ROWS, COLS), f32),
             dma((2, 8)), dma((2, 8)), dma((2, 8)), dma((2, 8)), dma((2, 2)), dma((2, 2)),
         ],
         compiler_params=pltpu.CompilerParams(
-            collective_id=0, has_side_effects=True, vmem_limit_bytes=32 << 20
+            collective_id=0, has_side_effects=True, vmem_limit_bytes=48 << 20
         ),
-    )(placed, neighbour, face, orient, density, momentum, energy, metrics, volume)
+    )(
+        *(
+            pltpu.with_memory_space_constraint(x, pltpu.HBM)
+            for x in (placed, neighbour.T, face.T, orient.T, density, momentum, energy, metrics, volume)
+        )
+    )
+    return pl.pallas_call(
+        hand_over,
+        out_shape=shapes,
+        in_specs=[inside] * 3,
+        out_specs=(anywhere,) * 3,
+        scratch_shapes=[dma((3,))],
+    )(*(pltpu.with_memory_space_constraint(x, pltpu.VMEM) for x in results))
 
 
 def solution(mesh):

time: 45.3 us -> 37 us (0.82)
  local copies, waits for them, and re-layouts: 7.68 us -> 0 us
    unnamed x22 -> x0, local copies, waits for them, and re-layouts: 7.68 us -> none
    pallas_call x1 -> x2, Pallas kernels: 36.6 us -> 36.2 us  [the longest x1 35.4 us: local(): pl.pallas_call(body, out_shape=shapes, in_specs=[anywhere] * 9, out_specs...]
where the time goes in v2:
time: 37 us; the launch traced here: 36.9 us
  Pallas kernels  36.2 us (98%)
  between operations  0.64 us (2%)
    pallas_call x1, Pallas kernels, local(): pl.pallas_call(body, out_shape=shapes, in_specs=[anywhere] * 9, out_specs...  35.4 us
    pallas_call x1, Pallas kernels, local(): pl.pallas_call(hand_over, out_shape=shapes, in_specs=[inside] * 3, out_sp...  0.8 us

profile of v2, /device:TPU:1, one launch (start us, length us, event | category | flops | bytes accessed | tf_op | source)
XLA Modules:
  0.0 36.9 jit_solution(13112268876063966328)
XLA Ops:
  0.6 35.4 %shard_map.112 = (f32[1,6,32,128]{3,2,1,0:T(8,128)S(1)}, f32[1,3,6,32,128]{4,3,2,1,0:T(8,128)S(1)}, f32[1,6,32,128]{3,2,1,0:T(8,128)S(1)}) custom-call(s32[32]{0:T(128)} %placed_hbm.1, s32[2,32]{1,0:T(2,128)} %bitcast.3, s32[2,32]{1,0:T(2,128)} %bitcast.4, s32[2,32]{1,0:T(2,128)} %bitcast.5, f32[1,6,32,128]{3,2,1,0:T(8,128)} %dens_hbm.1, ...), custom_call_target="tpu_custom_call" | custom-call | tf_op jit(solution)/shard_map/pallas_call | solution.py:386
  36.1 0.8 %shard_map.113 = (f32[1,6,32,128]{3,2,1,0:T(8,128)}, f32[1,3,6,32,128]{4,3,2,1,0:T(8,128)}, f32[1,6,32,128]{3,2,1,0:T(8,128)}) custom-call(f32[1,6,32,128]{3,2,1,0:T(8,128)S(1)} %get-tuple-element.6.d, f32[1,3,6,32,128]{4,3,2,1,0:T(8,128)S(1)} %get-tuple-element.7.m, f32[1,6,32,128]{3,2,1,0:T(8,128)S(1)} %get-tuple-element.8.e), custom_call_target="tpu_custom_call" | custom-call | tf_op jit(solution)/shard_map/pallas_call | solution.py:419

commit v3 on v2

v3 whole, which is shorter than its diff:
```python
import functools

import jax
import jax.numpy as jnp
from jax import lax
from jax.experimental import pallas as pl
from jax.experimental.pallas import tpu as pltpu
from jax.sharding import PartitionSpec as P

MESH = pl.DeviceIdType.MESH
pressure_factor = 0.4
viscosity = 0.05
conduction = 0.1
time_step = 0.03
ROWS, COLS, PLANES, CHUNK = 32, 128, 6, 8
Y, Z, CORES, IJ, BLOCKS = 4, 4, 2, 8, 32
LOW, HIGH = slice(6, 8), slice(40, 42)


def lanes(shape):
    return lax.broadcasted_iota(jnp.int32, shape, len(shape) - 1)


def rows_of(shape):
    return lax.broadcasted_iota(jnp.int32, shape, len(shape) - 2)


def shift_lanes(x, by):
    by = by % COLS
    return x if by == 0 else pltpu.roll(x, by, x.ndim - 1)


def primitives(rho, m1, m2, m3, energy, dt):
    inv = 1.0 / rho
    u1, u2, u3 = m1 * inv, m2 * inv, m3 * inv
    kinetic = 0.5 * (m1 * u1 + m2 * u2 + m3 * u3)
    p = pressure_factor * (energy - kinetic)
    head = energy + p
    soft = dt * viscosity / 12.0
    warm = dt * conduction / 12.0
    curved = (soft * u1, soft * u2, soft * u3, inv * (soft * kinetic + warm * p))
    return u1, u2, u3, p, head, curved


def flux(rho, m1, m2, m3, prim, gx, gy):
    u1, u2, u3, p, head, _ = prim
    speed = gx * u1 + gy * u2
    return (rho * speed, m1 * speed + gx * p, m2 * speed + gy * p, m3 * speed, head * speed)


def flux_planes(m1, m2, m3, prim):
    u1, u2, u3, p, head, _ = prim
    return (m3, m1 * u3, m2 * u3, m3 * u3 + p, head * u3)


def slope(b2, b1, a1, a2):
    return 8.0 * (a1 - b1) - (a2 - b2)


def curve(b2, b1, a1, a2):
    return 16.0 * (a1 + b1) - (a2 + b2)


def plane_shift(f, by):
    by = by % PLANES
    return jnp.concatenate([f[by:], f[:by]], axis=0)


def span(c):
    return slice(CHUNK + c * CHUNK, 2 * CHUNK + c * CHUNK)


def chunk_metrics(exm, c, dt):
    ax, ay, bx, by, v = (exm[n, span(c), :] for n in range(5))
    return (v * ax, v * ay, v * bx, v * by, (dt / 12.0) / v, ax * ax + ay * ay, bx * bx + by * by)


def before_ghosts(state, exm, fi, wi, part, dt, chunks):
    for c in chunks:
        gax, gay, gbx, gby, iv, rw, cw = chunk_metrics(exm, c, dt)
        center = -30.0 * (rw + cw + 1.0)
        rho, m1, m2, m3, energy = (state[ch, :, span(c), :] for ch in range(5))
        prim = primitives(rho, m1, m2, m3, energy, dt)
        curved = prim[5]
        inner = span(c + 1)
        for ch, f in enumerate(flux(rho, m1, m2, m3, prim, gax, gay)):
            fi[ch, :, inner, :] = f
        for n, w in enumerate(curved):
            wi[n, :, inner, :] = w
        fj = flux(rho, m1, m2, m3, prim, gbx, gby)
        fk = flux_planes(m1, m2, m3, prim)
        for ch in range(5):
            f, g = fj[ch], fk[ch]
            dj = slope(*(shift_lanes(f, by) for by in (2, 1, -1, -2)))
            dk = slope(*(plane_shift(g, by) for by in (-2, -1, 1, 2)))
            total = -(dj * iv) - (dt / 12.0) * dk
            if ch > 0:
                w = curved[ch - 1]
                sj = curve(*(shift_lanes(w, by) for by in (2, 1, -1, -2)))
                sk = curve(*(plane_shift(w, by) for by in (-2, -1, 1, 2)))
                total = total + cw * sj + sk + center * w
            part[ch, :, span(c), :] = total


def row_terms(exm, fi, wi, part, c, ch, dt):
    gax, gay, gbx, gby, iv, rw, cw = chunk_metrics(exm, c, dt)
    base = 2 * CHUNK + c * CHUNK
    di = slope(*(fi[ch, :, base + d : base + d + CHUNK, :] for d in (-2, -1, 1, 2)))
    total = part[ch, :, span(c), :] - di * iv
    if ch > 0:
        si = curve(*(wi[ch - 1, :, base + d : base + d + CHUNK, :] for d in (-2, -1, 1, 2)))
        total = total + rw * si
    return total


def edge_columns(edge, exm, c, ch, dt):
    at = lanes((CHUNK, COLS))
    border = (at < 2) | (at >= COLS - 2)
    gax, gay, gbx, gby, iv, rw, cw = chunk_metrics(exm, c, dt)
    terms = []
    for k in range(PLANES):
        term = -(shift_lanes(edge[ch, span(c), :], -8 * k - 4) * iv)
        if ch > 0:
            term = term + cw * shift_lanes(edge[4 + ch, span(c), :], -8 * k - 4)
        terms.append(jnp.where(border, term, 0.0))
    return jnp.stack(terms, axis=0)


def apart(a, b):
    third = jnp.where(lanes(a.shape) < 32, shift_lanes(a, -96), shift_lanes(b, 32))
    return [a, shift_lanes(a, -48), third, shift_lanes(b, -16), shift_lanes(b, -64)]


def spread(x):
    x = jnp.where((lanes(x.shape) & 63) < 8, x, 0.0)
    pair = x + shift_lanes(x, 8)
    return pair + shift_lanes(pair, 16) + shift_lanes(pair, 32)


def lines(own, ghost):
    near = (lanes(own.shape) & 7) < 4
    first = jnp.where(near, ghost, own)
    second = jnp.where(near, own, ghost)
    return jnp.where(lanes(own.shape) < 64, first, shift_lanes(second, 64))


def line_planes(x, by):
    m = lanes(x.shape) & 63
    if by > 0:
        return jnp.where(m < 48 - 8 * by, shift_lanes(x, -8 * by), shift_lanes(x, 48 - 8 * by))
    return jnp.where(m >= -8 * by, shift_lanes(x, -8 * by), shift_lanes(x, -48 - 8 * by))


def edge_terms(mine, theirs):
    upper = (lanes(mine[0].shape) & 7) >= 4
    out = []
    for n in range(9):
        h = theirs[n] - mine[n]
        high, low = jnp.where(upper, h, 0.0), jnp.where(upper, 0.0, h)
        if n < 5:
            left = 8.0 * shift_lanes(high, -1) - shift_lanes(high, -2)
            right = shift_lanes(low, 2) - 8.0 * shift_lanes(low, 1)
        else:
            left = 16.0 * shift_lanes(high, -1) - shift_lanes(high, -2)
            right = 16.0 * shift_lanes(low, 1) - shift_lanes(low, 2)
        out.append(jnp.where(upper, right, left))
    return out


def edge_values(fields, gx, gy, dt):
    rho, m1, m2, m3, energy = fields
    prim = primitives(rho, m1, m2, m3, energy, dt)
    return flux(rho, m1, m2, m3, prim, gx, gy) + prim[5]


def column_metric(c, e):
    return jnp.concatenate([shift_lanes(c, -32 * g - 8 * e) for g in range(4)], axis=0)


def line_section(own, ghost, lf, own_edge, ghost_edge, edge, dt):
    a, b, c = slice(0, 32), slice(32, 64), slice(64, 72)
    ob, gb = own[b, :], ghost[b, :]
    fields = [lines(o, g) for o, g in zip(apart(own[a, :], ob), apart(ghost[a, :], gb))]
    gbx, gby = (spread(lines(shift_lanes(ob, -n), shift_lanes(gb, -n))) for n in (112, 120))
    oc, gc = own[c, :], ghost[c, :]
    gax, gay, v = (spread(lines(column_metric(oc, e), column_metric(gc, e))) for e in range(3))
    rho, m1, m2, m3, energy = fields
    prim = primitives(rho, m1, m2, m3, energy, dt)
    curved = prim[5]
    for n, f in enumerate(flux(rho, m1, m2, m3, prim, gax, gay) + curved):
        lf[n, span(0).start : span(3).stop, :] = f
    h = (slice(72, 76), slice(76, 80), slice(80, 84))
    oa, ob, od = (own[n, :] for n in h)
    ga, gb, gd = (ghost[n, :] for n in h)
    mine, theirs = apart(oa, ob), apart(ga, gb)
    hax, hay = (spread(lines(shift_lanes(od, -n), shift_lanes(gd, -n))) for n in (0, 8))
    ends = [lines(o, g) for o, g in zip(mine, theirs)]
    end_prim = primitives(*ends, dt)
    for n, f in enumerate(flux(*ends[:4], end_prim, hax, hay) + end_prim[5]):
        lf[n, LOW, :] = f[0:2]
        lf[n, HIGH, :] = f[2:4]
    ends = edge_terms(
        edge_values(mine, *(spread(shift_lanes(ob, -n)) for n in (112, 120)), dt),
        edge_values(theirs, *(spread(shift_lanes(gb, -n)) for n in (112, 120)), dt),
    )
    for n, f in enumerate(ends):
        edge[n, LOW, :] = f[0:2]
        edge[n, HIGH, :] = f[2:4]
    inv = 1.0 / v
    iv = (dt / 12.0) * inv
    rw = (gax * gax + gay * gay) * (inv * inv)
    cw = (gbx * gbx + gby * gby) * (inv * inv)
    center = -30.0 * (rw + cw + 1.0)
    fj = flux(rho, m1, m2, m3, prim, gbx, gby)
    fk = flux_planes(m1, m2, m3, prim)
    near = (lanes((ROWS, COLS)) & 7) < 4
    for ch in range(7):
        if ch < 5:
            di = slope(*(lf[ch, CHUNK + d : CHUNK + d + ROWS, :] for d in (-2, -1, 1, 2)))
            dj = slope(*(shift_lanes(fj[ch], by) for by in (2, 1, -1, -2)))
            dk = slope(*(line_planes(fk[ch], by) for by in (-2, -1, 1, 2)))
            value = fields[ch] - (di + dj) * iv - (dt / 12.0) * dk
            if ch > 0:
                w = curved[ch - 1]
                si = curve(*(lf[4 + ch, CHUNK + d : CHUNK + d + ROWS, :] for d in (-2, -1, 1, 2)))
                sj = curve(*(shift_lanes(w, by) for by in (2, 1, -1, -2)))
                sk = curve(*(line_planes(w, by) for by in (-2, -1, 1, 2)))
                value = value + rw * si + cw * sj + sk + center * w
        else:
            value = (gbx, gby)[ch - 5]
        other = shift_lanes(value, 64)
        own_edge[ch] = jnp.where(near, other, value)
        ghost_edge[ch] = jnp.where(near, value, other)


def pack(ex, exm, strips, relay):
    at = lanes((ROWS, COLS)) >> 3
    inside = slice(CHUNK, CHUNK + ROWS)
    v = exm[4, inside, :]
    for half in range(2):
        acc = jnp.zeros((ROWS, COLS), jnp.float32)
        for n in range(16):
            q = 16 * half + n
            x = ex[q // 6, q % 6, inside, :] if q < 30 else v * exm[q - 28, inside, :]
            acc = jnp.where(at == n, shift_lanes(x, 4 + 8 * n), acc)
        strips[0, 32 * half : 32 * half + 32, :] = acc
    slot = lanes((CHUNK, COLS)) >> 3
    acc = jnp.zeros((CHUNK, COLS), jnp.float32)
    for g in range(4):
        part = exm[4, span(g), :]
        for e in range(3):
            x = part * exm[e, span(g), :] if e < 2 else part
            acc = jnp.where(slot == 4 * g + e, shift_lanes(x, 4 + 32 * g + 8 * e), acc)
    strips[0, 64:72, :] = acc
    for r in range(ROWS):
        for half in (0, 32):
            strips[1, half + 31 - r : half + 32 - r, :] = strips[0, half + r : half + r + 1, :]
    turned = jnp.where((lanes(acc.shape) & 32) == 0, shift_lanes(acc, 32), shift_lanes(acc, -32))
    turned = jnp.where((lanes(acc.shape) & 31) < 16, -turned, turned)
    for r in range(CHUNK):
        strips[1, 71 - r : 72 - r, :] = turned[r : r + 1, :]
    for side, r in ((0, 0), (1, ROWS - 2)):
        relay[side, 0:2, :] = strips[0, r : r + 2, :]
        relay[side, 2:4, :] = strips[0, 32 + r : 34 + r, :]
        relay[side, 4:6, :] = shift_lanes(acc[r % CHUNK : r % CHUNK + 2], -32 * (r // CHUNK))
        relay[side, 6:8, :] = jnp.zeros((2, COLS), jnp.float32)


def pack_ends(relay, arrived, strips, at_start, at_end):
    turn = lanes((1, COLS))
    signs = (
        jnp.where(turn >= 48, -1.0, 1.0),
        jnp.where(turn < 64, -1.0, 1.0),
        jnp.ones((1, COLS), jnp.float32),
    )
    for n in range(3):
        base = 72 + 4 * n
        for r in range(4):
            near = 2 * n + r % 2
            wall = 2 * n + 1 - r % 2
            side = r // 2
            mirror = relay[side, wall : wall + 1, :]
            if side == 0:
                row = jnp.where(at_start, signs[n] * mirror, arrived[side, near : near + 1, :])
            else:
                row = jnp.where(at_end, mirror, arrived[side, near : near + 1, :])
            strips[0, base + r : base + r + 1, :] = row
            strips[1, base + 3 - r : base + 4 - r, :] = -row if n == 2 else row
    for m in range(2):
        strips[m, 84:88, :] = jnp.zeros((4, COLS), jnp.float32)


def walls(state, at_start, at_end):
    for ch in range(5):
        sign = -1.0 if 1 <= ch <= 3 else 1.0
        for r in range(2):
            low, high = slice(7 - r, 8 - r), slice(40 + r, 41 + r)
            mirror = state[ch, :, 8 + r : 9 + r, :]
            state[ch, :, low, :] = jnp.where(at_start, sign * mirror, state[ch, :, low, :])
            mirror = state[ch, :, 39 - r : 40 - r, :]
            state[ch, :, high, :] = jnp.where(at_end, mirror, state[ch, :, high, :])


def metric_walls(exm, at_start, at_end):
    for r in range(2):
        low, high = slice(7 - r, 8 - r), slice(40 + r, 41 + r)
        exm[:, low, :] = jnp.where(at_start, exm[:, 8 + r : 9 + r, :], exm[:, low, :])
        exm[:, high, :] = jnp.where(at_end, exm[:, 39 - r : 40 - r, :], exm[:, high, :])


def halo_rows(state, exm, fi, wi, dt):
    for rows in (LOW, HIGH):
        rho, m1, m2, m3, energy = (state[ch, :, rows, :] for ch in range(5))
        v = exm[4, rows, :]
        prim = primitives(rho, m1, m2, m3, energy, dt)
        target = slice(rows.start + CHUNK, rows.stop + CHUNK)
        for ch, f in enumerate(flux(rho, m1, m2, m3, prim, v * exm[0, rows, :], v * exm[1, rows, :])):
            fi[ch, :, target, :] = f
        for n, w in enumerate(prim[5]):
            wi[n, :, target, :] = w


def flip(x):
    t = lanes(x.shape) & 7
    for d in (4, 2, 1):
        x = jnp.where((t & d) == 0, shift_lanes(x, -d), shift_lanes(x, d))
    return x


def peers_first(y, z, c, s):
    out = []
    for dz in range(Z):
        for m in range(2):
            blk = (y * Z + lax.rem(z + dz, Z)) * CORES + c
            out.append({"blk": blk, "ij": (IJ - 1 - s) if m else s})
    return out


def peers_second(y, z, c, s):
    out = []
    for dy in range(Y):
        for dc in range(2):
            blk = (lax.rem(y + dy, Y) * Z + z) * CORES + (1 - c if dc else c)
            out.append({"blk": blk, "ij": s})
    return out


def routes(placed, neighbour, face, orient, targets):
    ids = [placed[t["blk"]] for t in targets]
    wanted = [(b, f) for b in ids for f in range(2)]
    nids = [neighbour[f, b] for b, f in wanted]

    def find(p, found):
        held = placed[p]
        return tuple(jnp.where(n == held, p, a) for n, a in zip(nids, found))

    found = lax.fori_loop(0, BLOCKS, find, tuple(jnp.int32(0) for _ in nids))
    return [(q, face[f, b], orient[f, b]) for q, (b, f) in zip(found, wanted)]


def body(
    placed_hbm, neighbour_hbm, face_hbm, orient_hbm, dens_hbm, mom_hbm, ener_hbm, met_hbm, vol_hbm,
    out_d, out_m, out_e,
    placed, neighbour, face, orient, load,
    ex, exm, sec, fi, wi, part, edge, lf, own_edge, ghost_edge,
    strips, relay, arrived, got, both, picked, got2, ghost,
    send1, recv1, send_h, recv_h, send2, recv2, send_e, recv_e, send_r, recv_r, send_m, recv_m,
):
    inside = pl.ds(CHUNK, ROWS)
    fetch = [
        pltpu.make_async_copy(src, dst, load.at[n])
        for n, (src, dst) in enumerate(
            (
                (mom_hbm.at[0], ex.at[pl.ds(1, 3), :, inside]),
                (dens_hbm.at[0], ex.at[0, :, inside]),
                (ener_hbm.at[0], ex.at[4, :, inside]),
                (met_hbm.at[0], exm.at[pl.ds(0, 4), inside]),
                (vol_hbm.at[0], exm.at[4, inside]),
                (placed_hbm, placed),
                (neighbour_hbm, neighbour),
                (face_hbm, face),
                (orient_hbm, orient),
            )
        )
    ]
    for copy in fetch:
        copy.start()
    b, s = lax.axis_index("blk"), lax.axis_index("ij")
    c = lax.rem(b, CORES)
    z = lax.rem(b // CORES, Z)
    y = b // (CORES * Z)
    first, second = peers_first(y, z, c, s), peers_second(y, z, c, s)
    below = {"blk": b, "ij": lax.rem(s + IJ - 1, IJ)}
    above = {"blk": b, "ij": lax.rem(s + 1, IJ)}
    everyone = first[1:] + second[1:] + [below, above]
    barrier = pltpu.get_barrier_semaphore()
    for peer in everyone:
        pl.semaphore_signal(barrier, inc=1, device_id=peer, device_id_type=MESH)
    at_start, at_end = s == 0, s == IJ - 1
    for copy in fetch:
        copy.wait()
    pack(ex, exm, strips, relay)
    pl.semaphore_wait(barrier, len(everyone))

    def send(src, dst, out_sem, in_sem, peer):
        copy = pltpu.make_async_remote_copy(
            src_ref=src, dst_ref=dst, send_sem=out_sem, recv_sem=in_sem,
            device_id=peer, device_id_type=MESH,
        )
        copy.start()
        return copy

    main, ends = pl.ds(0, 72), pl.ds(72, 16)
    beside = (below, above)
    order = (2, 4, 1, 3, 5, 6, 7)
    edges = [
        send(relay.at[n], arrived.at[1 - n], send_e.at[n], recv_e.at[1 - n], beside[n]) for n in range(2)
    ]
    hop1 = {
        k: send(strips.at[k % 2, main], got.at[k, main], send1.at[k], recv1.at[k], first[k]) for k in order
    }
    slide = []
    for n in range(2):
        src, dst = pl.ds((CHUNK, ROWS)[n], CHUNK), pl.ds((CHUNK + ROWS, 0)[n], CHUNK)
        slide.append(send(exm.at[:, src], exm.at[:, dst], send_m.at[n], recv_m.at[1 - n], beside[n]))
        slide.append(send(ex.at[:, :, src], ex.at[:, :, dst], send_r.at[n], recv_r.at[1 - n], beside[n]))
    table = routes(placed, neighbour, face, orient, second)
    before_ghosts(ex, exm, fi, wi, part, time_step, range(4))
    for copy in edges:
        copy.wait_send()
    for n in range(2):
        pltpu.make_async_remote_copy(
            src_ref=relay.at[n], dst_ref=arrived.at[n], send_sem=send_e.at[n], recv_sem=recv_e.at[n],
            device_id=beside[n], device_id_type=MESH,
        ).wait_recv()
    pack_ends(relay, arrived, strips, at_start, at_end)
    hop_ends = {
        k: send(strips.at[k % 2, ends], got.at[k, ends], send_h.at[k], recv_h.at[k], first[k]) for k in order
    }
    main_sign = jnp.where((rows_of((72, COLS)) >= 32) & (rows_of((72, COLS)) < 64) & (lanes((72, COLS)) >= 112), -1.0, 1.0)
    ends_sign = jnp.where(
        (rows_of((16, COLS)) >= 4) & (rows_of((16, COLS)) < 8) & (lanes((16, COLS)) >= 112), -1.0, 1.0
    )
    for piece, sign, copies in ((slice(0, 72), main_sign, hop1), (slice(72, 88), ends_sign, hop_ends)):
        for k in (0, 1, 2, 3, 6, 7, 4, 5):
            if k > 0:
                copies[k].wait_recv()
                x = got[k, piece, :]
            else:
                x = strips[0, piece, :]
            both[k, piece, :] = x
            both[8 + k, piece, :] = flip(x) * sign
    near = (lanes((88, COLS)) & 7) < 4
    hop2 = []
    for k in (4, 5, 2, 3, 6, 7, 1, 0):
        parts = []
        for f in range(2):
            q, g, o = table[2 * k + f]
            dz = lax.rem(z - lax.rem(q // CORES, Z) + Z, Z)
            parts.append(both[jnp.where(g == f, 8, 0) + 2 * dz + o])
        message = jnp.where(near, parts[0], parts[1])
        if k == 0:
            got2[0] = message
        else:
            picked[k] = message
            hop2.append(send(picked.at[k], got2.at[k], send2.at[k], recv2.at[k], second[k]))
    for copy in slide:
        copy.wait_send()
    for n in range(2):
        dst = pl.ds((0, CHUNK + ROWS)[n], CHUNK)
        pltpu.make_async_remote_copy(
            src_ref=exm.at[:, dst], dst_ref=exm.at[:, dst], send_sem=send_m.at[n], recv_sem=recv_m.at[n],
            device_id=beside[n], device_id_type=MESH,
        ).wait_recv()
        pltpu.make_async_remote_copy(
            src_ref=ex.at[:, :, dst], dst_ref=ex.at[:, :, dst], send_sem=send_r.at[n], recv_sem=recv_r.at[n],
            device_id=beside[n], device_id_type=MESH,
        ).wait_recv()
    walls(ex, at_start, at_end)
    metric_walls(exm, at_start, at_end)
    before_ghosts(ex, exm, fi, wi, part, time_step, (-1, 4))
    for n in range(-1, 5):
        for ch in range(5):
            sec[ch, :, span(n), :] = ex[ch, :, span(n), :] + row_terms(exm, fi, wi, part, n, ch, time_step)
    for copy in hop2:
        copy.wait_recv()
    sides = []
    for f in range(2):
        q, g, o = table[f]
        dy = lax.rem(y - q // (CORES * Z) + Y, Y)
        dc = jnp.where(lax.rem(q, CORES) == c, 0, 1)
        sides.append(got2[2 * dy + dc])
    ghost[...] = jnp.where(near, sides[0], sides[1])
    line_section(strips.at[0], ghost, lf, own_edge, ghost_edge, edge, time_step)
    at = lanes((CHUNK, COLS))
    border = (at < 2) | (at >= COLS - 2)
    for ch in range(5):
        for n in range(4):
            rows = slice(n * CHUNK, (n + 1) * CHUNK)
            for k in range(PLANES):
                x = shift_lanes(own_edge[ch, rows, :], -8 * k - 4)
                sec[ch, k, span(n), :] = jnp.where(border, x, sec[ch, k, span(n), :])
        for n in (-1, 4):
            sec[ch, :, span(n), :] = sec[ch, :, span(n), :] + edge_columns(edge, exm, n, ch, time_step)
    walls(sec, at_start, at_end)
    half = 0.5 * time_step
    before_ghosts(sec, exm, fi, wi, part, half, range(4))
    halo_rows(sec, exm, fi, wi, half)
    changes = edge_terms(
        edge_values([own_edge[n] for n in range(5)], own_edge[5], own_edge[6], half),
        edge_values([ghost_edge[n] for n in range(5)], ghost_edge[5], ghost_edge[6], half),
    )
    for n, x in enumerate(changes):
        edge[n, CHUNK : CHUNK + ROWS, :] = x
    for n in range(4):
        rows = slice(n * CHUNK, (n + 1) * CHUNK)
        for ch in range(5):
            value = 0.5 * (ex[ch, :, span(n), :] + sec[ch, :, span(n), :])
            value = value + row_terms(exm, fi, wi, part, n, ch, half)
            value = value + edge_columns(edge, exm, n, ch, half)
            if ch == 0:
                out_d[0, :, rows, :] = value
            elif ch == 4:
                out_e[0, :, rows, :] = value
            else:
                out_m[0, ch - 1, :, rows, :] = value
    for copy in list(hop1.values()) + list(hop_ends.values()) + hop2:
        copy.wait_send()


def hand_over(d, m, e, out_d, out_m, out_e, sems):
    copies = [
        pltpu.make_async_copy(src, dst, sems.at[n])
        for n, (src, dst) in enumerate(((m, out_m), (d, out_d), (e, out_e)))
    ]
    for copy in copies:
        copy.start()
    for copy in copies:
        copy.wait()


def local(density, momentum, energy, metrics, volume, placed, neighbour, face, orient):
    smem, vmem, i32, f32 = pltpu.SMEM, pltpu.VMEM, jnp.int32, jnp.float32
    anywhere = pl.BlockSpec(memory_space=pltpu.HBM)
    inside = pl.BlockSpec(memory_space=pltpu.VMEM)
    dma = pltpu.SemaphoreType.DMA
    padded = ROWS + 2 * CHUNK
    shapes = tuple(jax.ShapeDtypeStruct(x.shape, f32) for x in (density, momentum, energy))
    results = pl.pallas_call(
        body,
        out_shape=shapes,
        in_specs=[anywhere] * 9,
        out_specs=(inside,) * 3,
        scratch_shapes=[
            smem((BLOCKS,), i32), smem((2, BLOCKS), i32), smem((2, BLOCKS), i32), smem((2, BLOCKS), i32),
            dma((9,)),
            vmem((5, PLANES, padded, COLS), f32),
            vmem((5, padded, COLS), f32),
            vmem((5, PLANES, padded, COLS), f32),
            vmem((5, PLANES, padded + 2 * CHUNK, COLS), f32),
            vmem((4, PLANES, padded + 2 * CHUNK, COLS), f32),
            vmem((5, PLANES, padded, COLS), f32),
            vmem((9, padded, COLS), f32),
            vmem((9, padded, COLS), f32),
            vmem((7, ROWS, COLS), f32),
            vmem((7, ROWS, COLS), f32),
            vmem((2, 88, COLS), f32),
            vmem((2, CHUNK, COLS), f32),
            vmem((2, CHUNK, COLS), f32),
            vmem((8, 88, COLS), f32),
            vmem((16, 88, COLS), f32),
            vmem((8, 88, COLS), f32),
            vmem((8, 88, COLS), f32),
            vmem((88, COLS), f32),
            dma((8,)), dma((8,)), dma((8,)), dma((8,)), dma((8,)), dma((8,)),
            dma((2,)), dma((2,)), dma((2,)), dma((2,)), dma((2,)), dma((2,)),
        ],
        compiler_params=pltpu.CompilerParams(
            collective_id=0, has_side_effects=True, vmem_limit_bytes=48 << 20
        ),
    )(
        *(
            pltpu.with_memory_space_constraint(x, pltpu.HBM)
            for x in (placed, neighbour.T, face.T, orient.T, density, momentum, energy, metrics, volume)
        )
    )
    return pl.pallas_call(
        hand_over,
        out_shape=shapes,
        in_specs=[inside] * 3,
        out_specs=(anywhere,) * 3,
        scratch_shapes=[dma((3,))],
    )(*(pltpu.with_memory_space_constraint(x, pltpu.VMEM) for x in results))


def solution(mesh):
    return jax.shard_map(
        local,
        mesh=mesh,
        in_specs=(
            P("blk", None, "ij", None),
            P("blk", None, None, "ij", None),
            P("blk", None, "ij", None),
            P("blk", None, "ij", None),
            P("blk", "ij", None),
            P(),
            P(),
            P(),
            P(),
        ),
        out_specs=(
            P("blk", None, "ij", None),
            P("blk", None, None, "ij", None),
            P("blk", None, "ij", None),
        ),
        check_vma=False,
    )
```

time: 37 us -> 37.9 us (1.024)
  Pallas kernels: 36.2 us -> 37.2 us
    pallas_call x1, Pallas kernels: 35.4 us -> 36.4 us  [local(): pl.pallas_call(body, out_shape=shapes, in_specs=[anywhere] * 9, out_specs...]
where the time goes in v3:
time: 37.9 us; the launch traced here: 37.8 us
  Pallas kernels  37.2 us (98%)
  between operations  0.64 us (2%)
    pallas_call x1, Pallas kernels, local(): pl.pallas_call(body, out_shape=shapes, in_specs=[anywhere] * 9, out_specs...  36.4 us
    pallas_call x1, Pallas kernels, local(): pl.pallas_call(hand_over, out_shape=shapes, in_specs=[inside] * 3, out_sp...  0.8 us

profile of v3, /device:TPU:1, one launch (start us, length us, event | category | flops | bytes accessed | tf_op | source)
XLA Modules:
  0.0 37.8 jit_solution(5054926282505204825)
XLA Ops:
  0.6 36.4 %shard_map.112 = (f32[1,6,32,128]{3,2,1,0:T(8,128)S(1)}, f32[1,3,6,32,128]{4,3,2,1,0:T(8,128)S(1)}, f32[1,6,32,128]{3,2,1,0:T(8,128)S(1)}) custom-call(s32[32]{0:T(128)} %placed_hbm.1, s32[2,32]{1,0:T(2,128)} %bitcast.3, s32[2,32]{1,0:T(2,128)} %bitcast.4, s32[2,32]{1,0:T(2,128)} %bitcast.5, f32[1,6,32,128]{3,2,1,0:T(8,128)} %dens_hbm.1, ...), custom_call_target="tpu_custom_call" | custom-call | tf_op jit(solution)/shard_map/pallas_call | solution.py:549
  37.0 0.8 %shard_map.113 = (f32[1,6,32,128]{3,2,1,0:T(8,128)}, f32[1,3,6,32,128]{4,3,2,1,0:T(8,128)}, f32[1,6,32,128]{3,2,1,0:T(8,128)}) custom-call(f32[1,6,32,128]{3,2,1,0:T(8,128)S(1)} %get-tuple-element.6.d, f32[1,3,6,32,128]{4,3,2,1,0:T(8,128)S(1)} %get-tuple-element.7.m, f32[1,6,32,128]{3,2,1,0:T(8,128)S(1)} %get-tuple-element.8.e), custom_call_target="tpu_custom_call" | custom-call | tf_op jit(solution)/shard_map/pallas_call | solution.py:587

commit v4 on v3

--- a/solution.py
+++ b/solution.py
@@ -363,8 +363,8 @@
     out_d, out_m, out_e,
     placed, neighbour, face, orient, load,
     ex, exm, sec, fi, wi, part, edge, lf, own_edge, ghost_edge,
-    strips, relay, arrived, got, both, picked, got2, ghost,
-    send1, recv1, send_h, recv_h, send2, recv2, send_e, recv_e, send_r, recv_r, send_m, recv_m,
+    strips, relay, arrived, got, both, picked, got2, both_e, picked_e, got2_e, ghost,
+    send1, recv1, send_h, recv_h, send2, recv2, send_f, recv_f, send_e, recv_e, send_r, recv_r, send_m, recv_m,
 ):
     inside = pl.ds(CHUNK, ROWS)
     fetch = [
@@ -419,11 +419,6 @@
     hop1 = {
         k: send(strips.at[k % 2, main], got.at[k, main], send1.at[k], recv1.at[k], first[k]) for k in order
     }
-    slide = []
-    for n in range(2):
-        src, dst = pl.ds((CHUNK, ROWS)[n], CHUNK), pl.ds((CHUNK + ROWS, 0)[n], CHUNK)
-        slide.append(send(exm.at[:, src], exm.at[:, dst], send_m.at[n], recv_m.at[1 - n], beside[n]))
-        slide.append(send(ex.at[:, :, src], ex.at[:, :, dst], send_r.at[n], recv_r.at[1 - n], beside[n]))
     table = routes(placed, neighbour, face, orient, second)
     before_ghosts(ex, exm, fi, wi, part, time_step, range(4))
     for copy in edges:
@@ -437,37 +432,47 @@
     hop_ends = {
         k: send(strips.at[k % 2, ends], got.at[k, ends], send_h.at[k], recv_h.at[k], first[k]) for k in order
     }
+    slide = []
+    for n in range(2):
+        src, dst = pl.ds((CHUNK, ROWS + 4)[n], 4), pl.ds((CHUNK + ROWS, 4)[n], 4)
+        slide.append(send(exm.at[:, src], exm.at[:, dst], send_m.at[n], recv_m.at[1 - n], beside[n]))
+        slide.append(send(ex.at[:, :, src], ex.at[:, :, dst], send_r.at[n], recv_r.at[1 - n], beside[n]))
     main_sign = jnp.where((rows_of((72, COLS)) >= 32) & (rows_of((72, COLS)) < 64) & (lanes((72, COLS)) >= 112), -1.0, 1.0)
     ends_sign = jnp.where(
         (rows_of((16, COLS)) >= 4) & (rows_of((16, COLS)) < 8) & (lanes((16, COLS)) >= 112), -1.0, 1.0
     )
-    for piece, sign, copies in ((slice(0, 72), main_sign, hop1), (slice(72, 88), ends_sign, hop_ends)):
+    slots = []
+    for q, g, o in table:
+        slots.append((lax.rem(z - lax.rem(q // CORES, Z) + Z, Z) * 2 + o, g))
+    near = (lanes((72, COLS)) & 7) < 4
+    hop2 = []
+    for piece, size, sign, copies, variants, chosen, landed, sems in (
+        (slice(0, 72), 72, main_sign, hop1, both, picked, got2, (send2, recv2)),
+        (slice(72, 88), 16, ends_sign, hop_ends, both_e, picked_e, got2_e, (send_f, recv_f)),
+    ):
         for k in (0, 1, 2, 3, 6, 7, 4, 5):
             if k > 0:
                 copies[k].wait_recv()
                 x = got[k, piece, :]
             else:
                 x = strips[0, piece, :]
-            both[k, piece, :] = x
-            both[8 + k, piece, :] = flip(x) * sign
-    near = (lanes((88, COLS)) & 7) < 4
-    hop2 = []
-    for k in (4, 5, 2, 3, 6, 7, 1, 0):
-        parts = []
-        for f in range(2):
-            q, g, o = table[2 * k + f]
-            dz = lax.rem(z - lax.rem(q // CORES, Z) + Z, Z)
-            parts.append(both[jnp.where(g == f, 8, 0) + 2 * dz + o])
-        message = jnp.where(near, parts[0], parts[1])
-        if k == 0:
-            got2[0] = message
-        else:
-            picked[k] = message
-            hop2.append(send(picked.at[k], got2.at[k], send2.at[k], recv2.at[k], second[k]))
+            variants[k] = x
+            variants[8 + k] = flip(x) * sign
+        for k in (4, 5, 2, 3, 6, 7, 1, 0):
+            parts = []
+            for f in range(2):
+                slot, g = slots[2 * k + f]
+                parts.append(variants[jnp.where(g == f, 8, 0) + slot])
+            message = jnp.where(near[:size], parts[0], parts[1])
+            if k == 0:
+                landed[0] = message
+            else:
+                chosen[k] = message
+                hop2.append(send(chosen.at[k], landed.at[k], sems[0].at[k], sems[1].at[k], second[k]))
     for copy in slide:
         copy.wait_send()
     for n in range(2):
-        dst = pl.ds((0, CHUNK + ROWS)[n], CHUNK)
+        dst = pl.ds((4, CHUNK + ROWS)[n], 4)
         pltpu.make_async_remote_copy(
             src_ref=exm.at[:, dst], dst_ref=exm.at[:, dst], send_sem=send_m.at[n], recv_sem=recv_m.at[n],
             device_id=beside[n], device_id_type=MESH,
@@ -482,15 +487,18 @@
     for n in range(-1, 5):
         for ch in range(5):
             sec[ch, :, span(n), :] = ex[ch, :, span(n), :] + row_terms(exm, fi, wi, part, n, ch, time_step)
-    for copy in hop2:
-        copy.wait_recv()
-    sides = []
+    origin = []
     for f in range(2):
         q, g, o = table[f]
         dy = lax.rem(y - q // (CORES * Z) + Y, Y)
         dc = jnp.where(lax.rem(q, CORES) == c, 0, 1)
-        sides.append(got2[2 * dy + dc])
-    ghost[...] = jnp.where(near, sides[0], sides[1])
+        origin.append(2 * dy + dc)
+    for copy in hop2[:7]:
+        copy.wait_recv()
+    ghost[0:72, :] = jnp.where(near, got2[origin[0]], got2[origin[1]])
+    for copy in hop2[7:]:
+        copy.wait_recv()
+    ghost[72:88, :] = jnp.where(near[:16], got2_e[origin[0]], got2_e[origin[1]])
     line_section(strips.at[0], ghost, lf, own_edge, ghost_edge, edge, time_step)
     at = lanes((CHUNK, COLS))
     border = (at < 2) | (at >= COLS - 2)
@@ -568,11 +576,14 @@
             vmem((2, CHUNK, COLS), f32),
             vmem((2, CHUNK, COLS), f32),
             vmem((8, 88, COLS), f32),
-            vmem((16, 88, COLS), f32),
-            vmem((8, 88, COLS), f32),
-            vmem((8, 88, COLS), f32),
+            vmem((16, 72, COLS), f32),
+            vmem((8, 72, COLS), f32),
+            vmem((8, 72, COLS), f32),
+            vmem((16, 16, COLS), f32),
+            vmem((8, 16, COLS), f32),
+            vmem((8, 16, COLS), f32),
             vmem((88, COLS), f32),
-            dma((8,)), dma((8,)), dma((8,)), dma((8,)), dma((8,)), dma((8,)),
+            dma((8,)), dma((8,)), dma((8,)), dma((8,)), dma((8,)), dma((8,)), dma((8,)), dma((8,)),
             dma((2,)), dma((2,)), dma((2,)), dma((2,)), dma((2,)), dma((2,)),
         ],
         compiler_params=pltpu.CompilerParams(

time: 37.9 us -> 34.3 us (0.905)
  Pallas kernels: 37.2 us -> 33.5 us
    pallas_call x1, Pallas kernels: 36.4 us -> 32.7 us  [local(): pl.pallas_call(body, out_shape=shapes, in_specs=[anywhere] * 9, out_specs...]
where the time goes in v4:
time: 34.3 us; the launch traced here: 34.2 us
  Pallas kernels  33.5 us (98%)
  between operations  0.64 us (2%)
    pallas_call x1, Pallas kernels, local(): pl.pallas_call(body, out_shape=shapes, in_specs=[anywhere] * 9, out_specs...  32.7 us
    pallas_call x1, Pallas kernels, local(): pl.pallas_call(hand_over, out_shape=shapes, in_specs=[inside] * 3, out_sp...  0.8 us

profile of v4, /device:TPU:1, one launch (start us, length us, event | category | flops | bytes accessed | tf_op | source)
XLA Modules:
  0.0 34.2 jit_solution(9902719230554444965)
XLA Ops:
  0.6 32.7 %shard_map.112 = (f32[1,6,32,128]{3,2,1,0:T(8,128)S(1)}, f32[1,3,6,32,128]{4,3,2,1,0:T(8,128)S(1)}, f32[1,6,32,128]{3,2,1,0:T(8,128)S(1)}) custom-call(s32[32]{0:T(128)} %placed_hbm.1, s32[2,32]{1,0:T(2,128)} %bitcast.3, s32[2,32]{1,0:T(2,128)} %bitcast.4, s32[2,32]{1,0:T(2,128)} %bitcast.5, f32[1,6,32,128]{3,2,1,0:T(8,128)} %dens_hbm.1, ...), custom_call_target="tpu_custom_call" | custom-call | tf_op jit(solution)/shard_map/pallas_call | solution.py:557
  33.4 0.8 %shard_map.113 = (f32[1,6,32,128]{3,2,1,0:T(8,128)}, f32[1,3,6,32,128]{4,3,2,1,0:T(8,128)}, f32[1,6,32,128]{3,2,1,0:T(8,128)}) custom-call(f32[1,6,32,128]{3,2,1,0:T(8,128)S(1)} %get-tuple-element.6.d, f32[1,3,6,32,128]{4,3,2,1,0:T(8,128)S(1)} %get-tuple-element.7.m, f32[1,6,32,128]{3,2,1,0:T(8,128)S(1)} %get-tuple-element.8.e), custom_call_target="tpu_custom_call" | custom-call | tf_op jit(solution)/shard_map/pallas_call | solution.py:598

commit v5 on v4

--- a/solution.py
+++ b/solution.py
@@ -113,19 +113,6 @@
     return total
 
 
-def edge_columns(edge, exm, c, ch, dt):
-    at = lanes((CHUNK, COLS))
-    border = (at < 2) | (at >= COLS - 2)
-    gax, gay, gbx, gby, iv, rw, cw = chunk_metrics(exm, c, dt)
-    terms = []
-    for k in range(PLANES):
-        term = -(shift_lanes(edge[ch, span(c), :], -8 * k - 4) * iv)
-        if ch > 0:
-            term = term + cw * shift_lanes(edge[4 + ch, span(c), :], -8 * k - 4)
-        terms.append(jnp.where(border, term, 0.0))
-    return jnp.stack(terms, axis=0)
-
-
 def apart(a, b):
     third = jnp.where(lanes(a.shape) < 32, shift_lanes(a, -96), shift_lanes(b, 32))
     return [a, shift_lanes(a, -48), third, shift_lanes(b, -16), shift_lanes(b, -64)]
@@ -177,7 +164,7 @@
     return jnp.concatenate([shift_lanes(c, -32 * g - 8 * e) for g in range(4)], axis=0)
 
 
-def line_section(own, ghost, lf, own_edge, ghost_edge, edge, dt):
+def line_section(own, ghost, lf, lines1, dt):
     a, b, c = slice(0, 32), slice(32, 64), slice(64, 72)
     ob, gb = own[b, :], ghost[b, :]
     fields = [lines(o, g) for o, g in zip(apart(own[a, :], ob), apart(ghost[a, :], gb))]
@@ -199,13 +186,10 @@
     for n, f in enumerate(flux(*ends[:4], end_prim, hax, hay) + end_prim[5]):
         lf[n, LOW, :] = f[0:2]
         lf[n, HIGH, :] = f[2:4]
-    ends = edge_terms(
+    terms = edge_terms(
         edge_values(mine, *(spread(shift_lanes(ob, -n)) for n in (112, 120)), dt),
         edge_values(theirs, *(spread(shift_lanes(gb, -n)) for n in (112, 120)), dt),
     )
-    for n, f in enumerate(ends):
-        edge[n, LOW, :] = f[0:2]
-        edge[n, HIGH, :] = f[2:4]
     inv = 1.0 / v
     iv = (dt / 12.0) * inv
     rw = (gax * gax + gay * gay) * (inv * inv)
@@ -213,24 +197,11 @@
     center = -30.0 * (rw + cw + 1.0)
     fj = flux(rho, m1, m2, m3, prim, gbx, gby)
     fk = flux_planes(m1, m2, m3, prim)
-    near = (lanes((ROWS, COLS)) & 7) < 4
-    for ch in range(7):
-        if ch < 5:
-            di = slope(*(lf[ch, CHUNK + d : CHUNK + d + ROWS, :] for d in (-2, -1, 1, 2)))
-            dj = slope(*(shift_lanes(fj[ch], by) for by in (2, 1, -1, -2)))
-            dk = slope(*(line_planes(fk[ch], by) for by in (-2, -1, 1, 2)))
-            value = fields[ch] - (di + dj) * iv - (dt / 12.0) * dk
-            if ch > 0:
-                w = curved[ch - 1]
-                si = curve(*(lf[4 + ch, CHUNK + d : CHUNK + d + ROWS, :] for d in (-2, -1, 1, 2)))
-                sj = curve(*(shift_lanes(w, by) for by in (2, 1, -1, -2)))
-                sk = curve(*(line_planes(w, by) for by in (-2, -1, 1, 2)))
-                value = value + rw * si + cw * sj + sk + center * w
-        else:
-            value = (gbx, gby)[ch - 5]
-        other = shift_lanes(value, 64)
-        own_edge[ch] = jnp.where(near, other, value)
-        ghost_edge[ch] = jnp.where(near, value, other)
+    for ch in range(5):
+        lines1[ch] = fields[ch] + line_rate(lf, fj, fk, curved, iv, rw, cw, center, ch, dt)
+    lines1[5] = gbx
+    lines1[6] = gby
+    return terms
 
 
 def pack(ex, exm, strips, relay):
@@ -320,6 +291,99 @@
             wi[n, :, target, :] = w
 
 
+def gather_lines(planes, shape):
+    at = lanes(shape) >> 3
+    acc = jnp.zeros(shape, jnp.float32)
+    for k, x in enumerate(planes):
+        acc = jnp.where(at == k, shift_lanes(x, 8 * k + 2), acc)
+        acc = jnp.where(at == 8 + k, shift_lanes(x, 8 * k - 58), acc)
+    return acc
+
+
+def metric_line(x):
+    return spread(jnp.where(lanes(x.shape) < 64, shift_lanes(x, 2), shift_lanes(x, -58)))
+
+
+def line_prepare(sec, exm, inner, inner_ends, metric, metric_ends):
+    inside = slice(CHUNK, CHUNK + ROWS)
+    for ch in range(5):
+        inner[ch] = gather_lines([sec[ch, k, inside, :] for k in range(PLANES)], (ROWS, COLS))
+    ax, ay, bx, by, v = (exm[n, inside, :] for n in range(5))
+    values = (v * ax, v * ay, v * bx, v * by, 1.0 / v, ax * ax + ay * ay, bx * bx + by * by)
+    for n, x in enumerate(values):
+        metric[n] = metric_line(x)
+    for side, rows in enumerate((LOW, HIGH)):
+        at = slice(2 * side, 2 * side + 2)
+        for ch in range(5):
+            inner_ends[ch, at, :] = gather_lines([sec[ch, k, rows, :] for k in range(PLANES)], (2, COLS))
+        ax, ay, bx, by, v = (exm[n, rows, :] for n in range(5))
+        for n, x in enumerate((v * ax, v * ay, 1.0 / v, bx * bx + by * by)):
+            metric_ends[n, at, :] = metric_line(x)
+
+
+def line_result(lines1, inner, inner_ends, metric, metric_ends, terms, lf, last, at_start, at_end, before, dt):
+    shape = (ROWS, COLS)
+    t, left = lanes(shape) & 7, lanes(shape) < 64
+    near = t < 4
+
+    def join(p, own):
+        return jnp.where(left, jnp.where(near, shift_lanes(p, -2), own), jnp.where(near, own, shift_lanes(p, 2)))
+
+    fields = [join(lines1[ch], inner[ch]) for ch in range(5)]
+    gbx, gby = join(lines1[5], metric[2]), join(lines1[6], metric[3])
+    gax, gay, inv, rw, cw = (metric[n] for n in (0, 1, 4, 5, 6))
+    prim = primitives(*fields, dt)
+    curved = prim[5]
+    for n, f in enumerate(flux(*fields[:4], prim, gax, gay) + curved):
+        lf[n, CHUNK : CHUNK + ROWS, :] = f
+    few = slice(0, 4)
+    te, le = lanes((4, COLS)) & 7, lanes((4, COLS)) < 64
+
+    def place(e):
+        here = jnp.where(le & ((te >> 1) == 1), shift_lanes(e, -2), 0.0)
+        return jnp.where(jnp.logical_not(le) & ((te >> 1) == 2), shift_lanes(e, 66), here)
+
+    inv_e, cw_e = metric_ends[2, few, :], metric_ends[3, few, :]
+    ends = []
+    for ch in range(5):
+        h = inner_ends[ch, few, :] - place(terms[ch]) * ((before / 12.0) * inv_e)
+        if ch > 0:
+            h = h + cw_e * place(terms[4 + ch])
+        sign = -1.0 if 1 <= ch <= 3 else 1.0
+        f = fields[ch]
+        wall = jnp.concatenate([sign * f[1:2], sign * f[0:1], f[31:32], f[30:31]], axis=0)
+        r = rows_of((4, COLS))
+        use = jnp.where(at_start, 1, 0) * jnp.where(r < 2, 1, 0) + jnp.where(at_end, 1, 0) * jnp.where(r >= 2, 1, 0)
+        ends.append(jnp.where(use > 0, wall, h))
+    end_prim = primitives(*ends, dt)
+    for n, f in enumerate(
+        flux(*ends[:4], end_prim, metric_ends[0, few, :], metric_ends[1, few, :]) + end_prim[5]
+    ):
+        lf[n, LOW, :] = f[0:2]
+        lf[n, HIGH, :] = f[2:4]
+    iv = (dt / 12.0) * inv
+    center = -30.0 * (rw + cw + 1.0)
+    fj = flux(*fields[:4], prim, gbx, gby)
+    fk = flux_planes(*fields[1:4], prim)
+    for ch in range(5):
+        value = 0.5 * fields[ch] + line_rate(lf, fj, fk, curved, iv, rw, cw, center, ch, dt)
+        last[ch] = jnp.where((t >= 2) & (t < 6), value, shift_lanes(value, -68))
+
+
+def line_rate(lf, fj, fk, curved, iv, rw, cw, center, ch, dt):
+    di = slope(*(lf[ch, CHUNK + d : CHUNK + d + ROWS, :] for d in (-2, -1, 1, 2)))
+    dj = slope(*(shift_lanes(fj[ch], by) for by in (2, 1, -1, -2)))
+    dk = slope(*(line_planes(fk[ch], by) for by in (-2, -1, 1, 2)))
+    value = -((di + dj) * iv) - (dt / 12.0) * dk
+    if ch > 0:
+        w = curved[ch - 1]
+        si = curve(*(lf[4 + ch, CHUNK + d : CHUNK + d + ROWS, :] for d in (-2, -1, 1, 2)))
+        sj = curve(*(shift_lanes(w, by) for by in (2, 1, -1, -2)))
+        sk = curve(*(line_planes(w, by) for by in (-2, -1, 1, 2)))
+        value = value + rw * si + cw * sj + sk + center * w
+    return value
+
+
 def flip(x):
     t = lanes(x.shape) & 7
     for d in (4, 2, 1):
@@ -362,7 +426,7 @@
     placed_hbm, neighbour_hbm, face_hbm, orient_hbm, dens_hbm, mom_hbm, ener_hbm, met_hbm, vol_hbm,
     out_d, out_m, out_e,
     placed, neighbour, face, orient, load,
-    ex, exm, sec, fi, wi, part, edge, lf, own_edge, ghost_edge,
+    ex, exm, sec, fi, wi, part, lf, lf2, lines1, last, inner, inner_ends, metric, metric_ends,
     strips, relay, arrived, got, both, picked, got2, both_e, picked_e, got2_e, ghost,
     send1, recv1, send_h, recv_h, send2, recv2, send_f, recv_f, send_e, recv_e, send_r, recv_r, send_m, recv_m,
 ):
@@ -487,6 +551,24 @@
     for n in range(-1, 5):
         for ch in range(5):
             sec[ch, :, span(n), :] = ex[ch, :, span(n), :] + row_terms(exm, fi, wi, part, n, ch, time_step)
+    walls(sec, at_start, at_end)
+    half = 0.5 * time_step
+    line_prepare(sec, exm, inner, inner_ends, metric, metric_ends)
+    before_ghosts(sec, exm, fi, wi, part, half, range(4))
+    halo_rows(sec, exm, fi, wi, half)
+
+    def output(ch, plane, rows):
+        if ch == 0:
+            return out_d.at[0, plane, rows]
+        if ch == 4:
+            return out_e.at[0, plane, rows]
+        return out_m.at[0, ch - 1, plane, rows]
+
+    for n in range(4):
+        rows = slice(n * CHUNK, (n + 1) * CHUNK)
+        for ch in range(5):
+            value = 0.5 * (ex[ch, :, span(n), :] + sec[ch, :, span(n), :])
+            output(ch, slice(None), rows)[...] = value + row_terms(exm, fi, wi, part, n, ch, half)
     origin = []
     for f in range(2):
         q, g, o = table[f]
@@ -499,39 +581,19 @@
     for copy in hop2[7:]:
         copy.wait_recv()
     ghost[72:88, :] = jnp.where(near[:16], got2_e[origin[0]], got2_e[origin[1]])
-    line_section(strips.at[0], ghost, lf, own_edge, ghost_edge, edge, time_step)
+    terms = line_section(strips.at[0], ghost, lf, lines1, time_step)
+    line_result(
+        lines1, inner, inner_ends, metric, metric_ends, terms, lf2, last, at_start, at_end, time_step, half
+    )
     at = lanes((CHUNK, COLS))
-    border = (at < 2) | (at >= COLS - 2)
+    border = (at < 4) | (at >= COLS - 4)
     for ch in range(5):
         for n in range(4):
             rows = slice(n * CHUNK, (n + 1) * CHUNK)
             for k in range(PLANES):
-                x = shift_lanes(own_edge[ch, rows, :], -8 * k - 4)
-                sec[ch, k, span(n), :] = jnp.where(border, x, sec[ch, k, span(n), :])
-        for n in (-1, 4):
-            sec[ch, :, span(n), :] = sec[ch, :, span(n), :] + edge_columns(edge, exm, n, ch, time_step)
-    walls(sec, at_start, at_end)
-    half = 0.5 * time_step
-    before_ghosts(sec, exm, fi, wi, part, half, range(4))
-    halo_rows(sec, exm, fi, wi, half)
-    changes = edge_terms(
-        edge_values([own_edge[n] for n in range(5)], own_edge[5], own_edge[6], half),
-        edge_values([ghost_edge[n] for n in range(5)], ghost_edge[5], ghost_edge[6], half),
-    )
-    for n, x in enumerate(changes):
-        edge[n, CHUNK : CHUNK + ROWS, :] = x
-    for n in range(4):
-        rows = slice(n * CHUNK, (n + 1) * CHUNK)
-        for ch in range(5):
-            value = 0.5 * (ex[ch, :, span(n), :] + sec[ch, :, span(n), :])
-            value = value + row_terms(exm, fi, wi, part, n, ch, half)
-            value = value + edge_columns(edge, exm, n, ch, half)
-            if ch == 0:
-                out_d[0, :, rows, :] = value
-            elif ch == 4:
-                out_e[0, :, rows, :] = value
-            else:
-                out_m[0, ch - 1, :, rows, :] = value
+                x = shift_lanes(last[ch, rows, :], -8 * k - 2) + 0.5 * ex[ch, k, span(n), :]
+                ref = output(ch, k, rows)
+                ref[...] = jnp.where(border, x, ref[...])
     for copy in list(hop1.values()) + list(hop_ends.values()) + hop2:
         copy.wait_send()
 
@@ -571,7 +633,11 @@
             vmem((9, padded, COLS), f32),
             vmem((9, padded, COLS), f32),
             vmem((7, ROWS, COLS), f32),
+            vmem((5, ROWS, COLS), f32),
+            vmem((5, ROWS, COLS), f32),
+            vmem((5, CHUNK, COLS), f32),
             vmem((7, ROWS, COLS), f32),
+            vmem((4, CHUNK, COLS), f32),
             vmem((2, 88, COLS), f32),
             vmem((2, CHUNK, COLS), f32),
             vmem((2, CHUNK, COLS), f32),

time: 34.3 us -> 33.2 us (0.968)
  Pallas kernels: 33.5 us -> 32.4 us
    pallas_call x1, Pallas kernels: 32.7 us -> 31.6 us  [local(): pl.pallas_call(body, out_shape=shapes, in_specs=[anywhere] * 9, out_specs...]
where the time goes in v5:
time: 33.2 us; the launch traced here: 33.1 us
  Pallas kernels  32.4 us (98%)
  between operations  0.64 us (2%)
    pallas_call x1, Pallas kernels, local(): pl.pallas_call(body, out_shape=shapes, in_specs=[anywhere] * 9, out_specs...  31.6 us
    pallas_call x1, Pallas kernels, local(): pl.pallas_call(hand_over, out_shape=shapes, in_specs=[inside] * 3, out_sp...  0.8 us

profile of v5, /device:TPU:1, one launch (start us, length us, event | category | flops | bytes accessed | tf_op | source)
XLA Modules:
  0.0 33.1 jit_solution(18254695690000793943)
XLA Ops:
  0.6 31.6 %shard_map.112 = (f32[1,6,32,128]{3,2,1,0:T(8,128)S(1)}, f32[1,3,6,32,128]{4,3,2,1,0:T(8,128)S(1)}, f32[1,6,32,128]{3,2,1,0:T(8,128)S(1)}) custom-call(s32[32]{0:T(128)} %placed_hbm.1, s32[2,32]{1,0:T(2,128)} %bitcast.3, s32[2,32]{1,0:T(2,128)} %bitcast.4, s32[2,32]{1,0:T(2,128)} %bitcast.5, f32[1,6,32,128]{3,2,1,0:T(8,128)} %dens_hbm.1, ...), custom_call_target="tpu_custom_call" | custom-call | tf_op jit(solution)/shard_map/pallas_call | solution.py:619
  32.3 0.8 %shard_map.113 = (f32[1,6,32,128]{3,2,1,0:T(8,128)}, f32[1,3,6,32,128]{4,3,2,1,0:T(8,128)}, f32[1,6,32,128]{3,2,1,0:T(8,128)}) custom-call(f32[1,6,32,128]{3,2,1,0:T(8,128)S(1)} %get-tuple-element.6.d, f32[1,3,6,32,128]{4,3,2,1,0:T(8,128)S(1)} %get-tuple-element.7.m, f32[1,6,32,128]{3,2,1,0:T(8,128)S(1)} %get-tuple-element.8.e), custom_call_target="tpu_custom_call" | custom-call | tf_op jit(solution)/shard_map/pallas_call | solution.py:664

commit v6 on v5

--- a/solution.py
+++ b/solution.py
@@ -164,44 +164,59 @@
     return jnp.concatenate([shift_lanes(c, -32 * g - 8 * e) for g in range(4)], axis=0)
 
 
-def line_section(own, ghost, lf, lines1, dt):
-    a, b, c = slice(0, 32), slice(32, 64), slice(64, 72)
-    ob, gb = own[b, :], ghost[b, :]
-    fields = [lines(o, g) for o, g in zip(apart(own[a, :], ob), apart(ghost[a, :], gb))]
-    gbx, gby = (spread(lines(shift_lanes(ob, -n), shift_lanes(gb, -n))) for n in (112, 120))
-    oc, gc = own[c, :], ghost[c, :]
-    gax, gay, v = (spread(lines(column_metric(oc, e), column_metric(gc, e))) for e in range(3))
-    rho, m1, m2, m3, energy = fields
-    prim = primitives(rho, m1, m2, m3, energy, dt)
+def line_own(own, held, held_ends, dt):
+    oa, ob, oc = own[0:32, :], own[32:64, :], own[64:72, :]
+    for n, x in enumerate(apart(oa, ob)):
+        held[n] = x
+    held[5], held[6] = shift_lanes(ob, -112), shift_lanes(ob, -120)
+    for e in range(3):
+        held[7 + e] = column_metric(oc, e)
+    few = slice(0, 4)
+    oa, ob, od = own[72:76, :], own[76:80, :], own[80:84, :]
+    mine = apart(oa, ob)
+    values = edge_values(mine, *(spread(shift_lanes(ob, -n)) for n in (112, 120)), dt)
+    for n, x in enumerate(tuple(mine) + (od, shift_lanes(od, -8)) + tuple(values)):
+        held_ends[n, few, :] = x
+
+
+def section_main(ghost, held, lf, lines1, keep, dt):
+    ga, gb, gc = ghost[0:32, :], ghost[32:64, :], ghost[64:72, :]
+    fields = [lines(held[n], x) for n, x in enumerate(apart(ga, gb))]
+    gbx, gby = (spread(lines(held[5 + n], shift_lanes(gb, -112 - 8 * n))) for n in range(2))
+    gax, gay, v = (spread(lines(held[7 + e], column_metric(gc, e))) for e in range(3))
+    prim = primitives(*fields, dt)
     curved = prim[5]
-    for n, f in enumerate(flux(rho, m1, m2, m3, prim, gax, gay) + curved):
-        lf[n, span(0).start : span(3).stop, :] = f
-    h = (slice(72, 76), slice(76, 80), slice(80, 84))
-    oa, ob, od = (own[n, :] for n in h)
-    ga, gb, gd = (ghost[n, :] for n in h)
-    mine, theirs = apart(oa, ob), apart(ga, gb)
-    hax, hay = (spread(lines(shift_lanes(od, -n), shift_lanes(gd, -n))) for n in (0, 8))
-    ends = [lines(o, g) for o, g in zip(mine, theirs)]
-    end_prim = primitives(*ends, dt)
-    for n, f in enumerate(flux(*ends[:4], end_prim, hax, hay) + end_prim[5]):
-        lf[n, LOW, :] = f[0:2]
-        lf[n, HIGH, :] = f[2:4]
-    terms = edge_terms(
-        edge_values(mine, *(spread(shift_lanes(ob, -n)) for n in (112, 120)), dt),
-        edge_values(theirs, *(spread(shift_lanes(gb, -n)) for n in (112, 120)), dt),
-    )
+    for n, f in enumerate(flux(*fields[:4], prim, gax, gay) + curved):
+        lf[n, CHUNK : CHUNK + ROWS, :] = f
     inv = 1.0 / v
     iv = (dt / 12.0) * inv
     rw = (gax * gax + gay * gay) * (inv * inv)
     cw = (gbx * gbx + gby * gby) * (inv * inv)
     center = -30.0 * (rw + cw + 1.0)
-    fj = flux(rho, m1, m2, m3, prim, gbx, gby)
-    fk = flux_planes(m1, m2, m3, prim)
+    fj = flux(*fields[:4], prim, gbx, gby)
+    fk = flux_planes(*fields[1:4], prim)
     for ch in range(5):
-        lines1[ch] = fields[ch] + line_rate(lf, fj, fk, curved, iv, rw, cw, center, ch, dt)
-    lines1[5] = gbx
-    lines1[6] = gby
-    return terms
+        lines1[ch] = fields[ch] + cross_rate(fj, fk, curved, iv, cw, center, ch, dt)
+    lines1[5], lines1[6] = gbx, gby
+    keep[0], keep[1] = iv, rw
+
+
+def section_ends(ghost, held_ends, lf, lines1, keep, dt):
+    few = slice(0, 4)
+    ga, gb, gd = ghost[72:76, :], ghost[76:80, :], ghost[80:84, :]
+    theirs = apart(ga, gb)
+    hax, hay = (spread(lines(held_ends[5 + n, few, :], shift_lanes(gd, -8 * n))) for n in range(2))
+    ends = [lines(held_ends[n, few, :], x) for n, x in enumerate(theirs)]
+    prim = primitives(*ends, dt)
+    for n, f in enumerate(flux(*ends[:4], prim, hax, hay) + prim[5]):
+        lf[n, LOW, :] = f[0:2]
+        lf[n, HIGH, :] = f[2:4]
+    for ch in range(5):
+        lines1[ch] = lines1[ch] + row_rate(lf, keep[0], keep[1], ch)
+    return edge_terms(
+        [held_ends[7 + n, few, :] for n in range(9)],
+        edge_values(theirs, *(spread(shift_lanes(gb, -n)) for n in (112, 120)), dt),
+    )
 
 
 def pack(ex, exm, strips, relay):
@@ -366,21 +381,26 @@
     fj = flux(*fields[:4], prim, gbx, gby)
     fk = flux_planes(*fields[1:4], prim)
     for ch in range(5):
-        value = 0.5 * fields[ch] + line_rate(lf, fj, fk, curved, iv, rw, cw, center, ch, dt)
+        value = 0.5 * fields[ch] + row_rate(lf, iv, rw, ch) + cross_rate(fj, fk, curved, iv, cw, center, ch, dt)
         last[ch] = jnp.where((t >= 2) & (t < 6), value, shift_lanes(value, -68))
 
 
-def line_rate(lf, fj, fk, curved, iv, rw, cw, center, ch, dt):
-    di = slope(*(lf[ch, CHUNK + d : CHUNK + d + ROWS, :] for d in (-2, -1, 1, 2)))
+def row_rate(lf, iv, rw, ch):
+    value = -(slope(*(lf[ch, CHUNK + d : CHUNK + d + ROWS, :] for d in (-2, -1, 1, 2))) * iv)
+    if ch > 0:
+        value = value + rw * curve(*(lf[4 + ch, CHUNK + d : CHUNK + d + ROWS, :] for d in (-2, -1, 1, 2)))
+    return value
+
+
+def cross_rate(fj, fk, curved, iv, cw, center, ch, dt):
     dj = slope(*(shift_lanes(fj[ch], by) for by in (2, 1, -1, -2)))
     dk = slope(*(line_planes(fk[ch], by) for by in (-2, -1, 1, 2)))
-    value = -((di + dj) * iv) - (dt / 12.0) * dk
+    value = -(dj * iv) - (dt / 12.0) * dk
     if ch > 0:
         w = curved[ch - 1]
-        si = curve(*(lf[4 + ch, CHUNK + d : CHUNK + d + ROWS, :] for d in (-2, -1, 1, 2)))
         sj = curve(*(shift_lanes(w, by) for by in (2, 1, -1, -2)))
         sk = curve(*(line_planes(w, by) for by in (-2, -1, 1, 2)))
-        value = value + rw * si + cw * sj + sk + center * w
+        value = value + cw * sj + sk + center * w
     return value
 
 
@@ -427,6 +447,7 @@
     out_d, out_m, out_e,
     placed, neighbour, face, orient, load,
     ex, exm, sec, fi, wi, part, lf, lf2, lines1, last, inner, inner_ends, metric, metric_ends,
+    held, held_ends, keep,
     strips, relay, arrived, got, both, picked, got2, both_e, picked_e, got2_e, ghost,
     send1, recv1, send_h, recv_h, send2, recv2, send_f, recv_f, send_e, recv_e, send_r, recv_r, send_m, recv_m,
 ):
@@ -575,13 +596,15 @@
         dy = lax.rem(y - q // (CORES * Z) + Y, Y)
         dc = jnp.where(lax.rem(q, CORES) == c, 0, 1)
         origin.append(2 * dy + dc)
+    line_own(strips.at[0], held, held_ends, time_step)
     for copy in hop2[:7]:
         copy.wait_recv()
     ghost[0:72, :] = jnp.where(near, got2[origin[0]], got2[origin[1]])
+    section_main(ghost, held, lf, lines1, keep, time_step)
     for copy in hop2[7:]:
         copy.wait_recv()
     ghost[72:88, :] = jnp.where(near[:16], got2_e[origin[0]], got2_e[origin[1]])
-    terms = line_section(strips.at[0], ghost, lf, lines1, time_step)
+    terms = section_ends(ghost, held_ends, lf, lines1, keep, time_step)
     line_result(
         lines1, inner, inner_ends, metric, metric_ends, terms, lf2, last, at_start, at_end, time_step, half
     )
@@ -638,6 +661,9 @@
             vmem((5, CHUNK, COLS), f32),
             vmem((7, ROWS, COLS), f32),
             vmem((4, CHUNK, COLS), f32),
+            vmem((10, ROWS, COLS), f32),
+            vmem((16, CHUNK, COLS), f32),
+            vmem((2, ROWS, COLS), f32),
             vmem((2, 88, COLS), f32),
             vmem((2, CHUNK, COLS), f32),
             vmem((2, CHUNK, COLS), f32),

time: 33.2 us -> 31.7 us (0.955)
  Pallas kernels: 32.4 us -> 30.9 us
    pallas_call x1, Pallas kernels: 31.6 us -> 30.1 us  [local(): pl.pallas_call(body, out_shape=shapes, in_specs=[anywhere] * 9, out_specs...]
where the time goes in v6:
time: 31.7 us; the launch traced here: 31.6 us
  Pallas kernels  30.9 us (97%)
  between operations  0.64 us (2%)
    pallas_call x1, Pallas kernels, local(): pl.pallas_call(body, out_shape=shapes, in_specs=[anywhere] * 9, out_specs...  30.1 us
    pallas_call x1, Pallas kernels, local(): pl.pallas_call(hand_over, out_shape=shapes, in_specs=[inside] * 3, out_sp...  0.8 us

profile of v6, /device:TPU:1, one launch (start us, length us, event | category | flops | bytes accessed | tf_op | source)
XLA Modules:
  0.0 31.6 jit_solution(5673836633787066713)
XLA Ops:
  0.6 30.1 %shard_map.112 = (f32[1,6,32,128]{3,2,1,0:T(8,128)S(1)}, f32[1,3,6,32,128]{4,3,2,1,0:T(8,128)S(1)}, f32[1,6,32,128]{3,2,1,0:T(8,128)S(1)}) custom-call(s32[32]{0:T(128)} %placed_hbm.1, s32[2,32]{1,0:T(2,128)} %bitcast.3, s32[2,32]{1,0:T(2,128)} %bitcast.4, s32[2,32]{1,0:T(2,128)} %bitcast.5, f32[1,6,32,128]{3,2,1,0:T(8,128)} %dens_hbm.1, ...), custom_call_target="tpu_custom_call" | custom-call | tf_op jit(solution)/shard_map/pallas_call | solution.py:642
  30.8 0.8 %shard_map.113 = (f32[1,6,32,128]{3,2,1,0:T(8,128)}, f32[1,3,6,32,128]{4,3,2,1,0:T(8,128)}, f32[1,6,32,128]{3,2,1,0:T(8,128)}) custom-call(f32[1,6,32,128]{3,2,1,0:T(8,128)S(1)} %get-tuple-element.6.d, f32[1,3,6,32,128]{4,3,2,1,0:T(8,128)S(1)} %get-tuple-element.7.m, f32[1,6,32,128]{3,2,1,0:T(8,128)S(1)} %get-tuple-element.8.e), custom_call_target="tpu_custom_call" | custom-call | tf_op jit(solution)/shard_map/pallas_call | solution.py:690

commit v7 on v6

--- a/solution.py
+++ b/solution.py
@@ -238,6 +238,15 @@
             x = part * exm[e, span(g), :] if e < 2 else part
             acc = jnp.where(slot == 4 * g + e, shift_lanes(x, 4 + 32 * g + 8 * e), acc)
     strips[0, 64:72, :] = acc
+    for side, r in ((0, 0), (1, ROWS - 2)):
+        relay[side, 0:2, :] = strips[0, r : r + 2, :]
+        relay[side, 2:4, :] = strips[0, 32 + r : 34 + r, :]
+        relay[side, 4:6, :] = shift_lanes(acc[r % CHUNK : r % CHUNK + 2], -32 * (r // CHUNK))
+        relay[side, 6:8, :] = jnp.zeros((2, COLS), jnp.float32)
+    return acc
+
+
+def turn_strips(strips, acc):
     for r in range(ROWS):
         for half in (0, 32):
             strips[1, half + 31 - r : half + 32 - r, :] = strips[0, half + r : half + r + 1, :]
@@ -245,11 +254,6 @@
     turned = jnp.where((lanes(acc.shape) & 31) < 16, -turned, turned)
     for r in range(CHUNK):
         strips[1, 71 - r : 72 - r, :] = turned[r : r + 1, :]
-    for side, r in ((0, 0), (1, ROWS - 2)):
-        relay[side, 0:2, :] = strips[0, r : r + 2, :]
-        relay[side, 2:4, :] = strips[0, 32 + r : 34 + r, :]
-        relay[side, 4:6, :] = shift_lanes(acc[r % CHUNK : r % CHUNK + 2], -32 * (r // CHUNK))
-        relay[side, 6:8, :] = jnp.zeros((2, COLS), jnp.float32)
 
 
 def pack_ends(relay, arrived, strips, at_start, at_end):
@@ -404,27 +408,33 @@
     return value
 
 
-def flip(x):
+def exchange_lanes(x, distances):
     t = lanes(x.shape) & 7
-    for d in (4, 2, 1):
+    for d in distances:
         x = jnp.where((t & d) == 0, shift_lanes(x, -d), shift_lanes(x, d))
     return x
 
 
+def settle(x, sign, table):
+    same = [jnp.where(table[f][1] == f, 1, 0) for f in range(2)]
+    turned = jnp.where((lanes(x.shape) & 7) < 4, same[0], same[1]) > 0
+    return jnp.where(turned, exchange_lanes(x, (2, 1)) * sign, x)
+
+
 def peers_first(y, z, c, s):
     out = []
-    for dz in range(Z):
+    for dy in range(Y):
         for m in range(2):
-            blk = (y * Z + lax.rem(z + dz, Z)) * CORES + c
+            blk = (lax.rem(y + dy, Y) * Z + z) * CORES + c
             out.append({"blk": blk, "ij": (IJ - 1 - s) if m else s})
     return out
 
 
 def peers_second(y, z, c, s):
     out = []
-    for dy in range(Y):
+    for dz in range(Z):
         for dc in range(2):
-            blk = (lax.rem(y + dy, Y) * Z + z) * CORES + (1 - c if dc else c)
+            blk = (y * Z + lax.rem(z + dz, Z)) * CORES + (1 - c if dc else c)
             out.append({"blk": blk, "ij": s})
     return out
 
@@ -444,9 +454,9 @@
 
 def body(
     placed_hbm, neighbour_hbm, face_hbm, orient_hbm, dens_hbm, mom_hbm, ener_hbm, met_hbm, vol_hbm,
-    out_d, out_m, out_e,
+    out_d, out_m, out_e, last,
     placed, neighbour, face, orient, load,
-    ex, exm, sec, fi, wi, part, lf, lf2, lines1, last, inner, inner_ends, metric, metric_ends,
+    ex, exm, sec, fi, wi, part, lf, lf2, lines1, inner, inner_ends, metric, metric_ends,
     held, held_ends, keep,
     strips, relay, arrived, got, both, picked, got2, both_e, picked_e, got2_e, ghost,
     send1, recv1, send_h, recv_h, send2, recv2, send_f, recv_f, send_e, recv_e, send_r, recv_r, send_m, recv_m,
@@ -482,9 +492,9 @@
     for peer in everyone:
         pl.semaphore_signal(barrier, inc=1, device_id=peer, device_id_type=MESH)
     at_start, at_end = s == 0, s == IJ - 1
-    for copy in fetch:
+    for copy in fetch[:5]:
         copy.wait()
-    pack(ex, exm, strips, relay)
+    acc = pack(ex, exm, strips, relay)
     pl.semaphore_wait(barrier, len(everyone))
 
     def send(src, dst, out_sem, in_sem, peer):
@@ -501,9 +511,13 @@
     edges = [
         send(relay.at[n], arrived.at[1 - n], send_e.at[n], recv_e.at[1 - n], beside[n]) for n in range(2)
     ]
-    hop1 = {
-        k: send(strips.at[k % 2, main], got.at[k, main], send1.at[k], recv1.at[k], first[k]) for k in order
-    }
+    hop1 = {}
+    for k in (4, 2, 6, 5, 3, 7, 1):
+        if k == 5:
+            turn_strips(strips, acc)
+        hop1[k] = send(strips.at[k % 2, main], got.at[k, main], send1.at[k], recv1.at[k], first[k])
+    for copy in fetch[5:]:
+        copy.wait()
     table = routes(placed, neighbour, face, orient, second)
     before_ghosts(ex, exm, fi, wi, part, time_step, range(4))
     for copy in edges:
@@ -528,12 +542,12 @@
     )
     slots = []
     for q, g, o in table:
-        slots.append((lax.rem(z - lax.rem(q // CORES, Z) + Z, Z) * 2 + o, g))
+        slots.append((lax.rem(y - q // (CORES * Z) + Y, Y) * 2 + o, g))
     near = (lanes((72, COLS)) & 7) < 4
     hop2 = []
-    for piece, size, sign, copies, variants, chosen, landed, sems in (
-        (slice(0, 72), 72, main_sign, hop1, both, picked, got2, (send2, recv2)),
-        (slice(72, 88), 16, ends_sign, hop_ends, both_e, picked_e, got2_e, (send_f, recv_f)),
+    for piece, size, copies, variants, chosen, landed, sems in (
+        (slice(0, 72), 72, hop1, both, picked, got2, (send2, recv2)),
+        (slice(72, 88), 16, hop_ends, both_e, picked_e, got2_e, (send_f, recv_f)),
     ):
         for k in (0, 1, 2, 3, 6, 7, 4, 5):
             if k > 0:
@@ -542,7 +556,7 @@
             else:
                 x = strips[0, piece, :]
             variants[k] = x
-            variants[8 + k] = flip(x) * sign
+            variants[8 + k] = exchange_lanes(x, (4,))
         for k in (4, 5, 2, 3, 6, 7, 1, 0):
             parts = []
             for f in range(2):
@@ -589,45 +603,44 @@
         rows = slice(n * CHUNK, (n + 1) * CHUNK)
         for ch in range(5):
             value = 0.5 * (ex[ch, :, span(n), :] + sec[ch, :, span(n), :])
-            output(ch, slice(None), rows)[...] = value + row_terms(exm, fi, wi, part, n, ch, half)
+            value = value + row_terms(exm, fi, wi, part, n, ch, half)
+            at = lanes(value.shape)
+            border = (at < 4) | (at >= COLS - 4)
+            output(ch, slice(None), rows)[...] = jnp.where(border, 0.5 * ex[ch, :, span(n), :], value)
     origin = []
     for f in range(2):
         q, g, o = table[f]
-        dy = lax.rem(y - q // (CORES * Z) + Y, Y)
+        dz = lax.rem(z - lax.rem(q // CORES, Z) + Z, Z)
         dc = jnp.where(lax.rem(q, CORES) == c, 0, 1)
-        origin.append(2 * dy + dc)
+        origin.append(2 * dz + dc)
     line_own(strips.at[0], held, held_ends, time_step)
     for copy in hop2[:7]:
         copy.wait_recv()
-    ghost[0:72, :] = jnp.where(near, got2[origin[0]], got2[origin[1]])
+    ghost[0:72, :] = settle(jnp.where(near, got2[origin[0]], got2[origin[1]]), main_sign, table)
     section_main(ghost, held, lf, lines1, keep, time_step)
     for copy in hop2[7:]:
         copy.wait_recv()
-    ghost[72:88, :] = jnp.where(near[:16], got2_e[origin[0]], got2_e[origin[1]])
+    ghost[72:88, :] = settle(jnp.where(near[:16], got2_e[origin[0]], got2_e[origin[1]]), ends_sign, table)
     terms = section_ends(ghost, held_ends, lf, lines1, keep, time_step)
     line_result(
         lines1, inner, inner_ends, metric, metric_ends, terms, lf2, last, at_start, at_end, time_step, half
     )
-    at = lanes((CHUNK, COLS))
-    border = (at < 4) | (at >= COLS - 4)
-    for ch in range(5):
-        for n in range(4):
-            rows = slice(n * CHUNK, (n + 1) * CHUNK)
-            for k in range(PLANES):
-                x = shift_lanes(last[ch, rows, :], -8 * k - 2) + 0.5 * ex[ch, k, span(n), :]
-                ref = output(ch, k, rows)
-                ref[...] = jnp.where(border, x, ref[...])
     for copy in list(hop1.values()) + list(hop_ends.values()) + hop2:
         copy.wait_send()
 
 
-def hand_over(d, m, e, out_d, out_m, out_e, sems):
-    copies = [
-        pltpu.make_async_copy(src, dst, sems.at[n])
-        for n, (src, dst) in enumerate(((m, out_m), (d, out_d), (e, out_e)))
-    ]
-    for copy in copies:
-        copy.start()
+def hand_over(d, m, e, last, out_d, out_m, out_e, result, sems):
+    at = lanes((ROWS, COLS))
+    border = (at < 4) | (at >= COLS - 4)
+    copies = []
+    for ch in (1, 2, 3, 0, 4):
+        source = d.at[0] if ch == 0 else e.at[0] if ch == 4 else m.at[0, ch - 1]
+        target = out_d.at[0] if ch == 0 else out_e.at[0] if ch == 4 else out_m.at[0, ch - 1]
+        for k in range(PLANES):
+            x = shift_lanes(last[ch], -8 * k - 2)
+            result[ch, k] = source[k] + jnp.where(border, x, 0.0)
+        copies.append(pltpu.make_async_copy(result.at[ch], target, sems.at[ch]))
+        copies[-1].start()
     for copy in copies:
         copy.wait()
 
@@ -641,9 +654,9 @@
     shapes = tuple(jax.ShapeDtypeStruct(x.shape, f32) for x in (density, momentum, energy))
     results = pl.pallas_call(
         body,
-        out_shape=shapes,
+        out_shape=shapes + (jax.ShapeDtypeStruct((5, ROWS, COLS), f32),),
         in_specs=[anywhere] * 9,
-        out_specs=(inside,) * 3,
+        out_specs=(inside,) * 4,
         scratch_shapes=[
             smem((BLOCKS,), i32), smem((2, BLOCKS), i32), smem((2, BLOCKS), i32), smem((2, BLOCKS), i32),
             dma((9,)),
@@ -656,7 +669,6 @@
             vmem((9, padded, COLS), f32),
             vmem((9, padded, COLS), f32),
             vmem((7, ROWS, COLS), f32),
-            vmem((5, ROWS, COLS), f32),
             vmem((5, ROWS, COLS), f32),
             vmem((5, CHUNK, COLS), f32),
             vmem((7, ROWS, COLS), f32),
@@ -690,9 +702,9 @@
     return pl.pallas_call(
         hand_over,
         out_shape=shapes,
-        in_specs=[inside] * 3,
+        in_specs=[inside] * 4,
         out_specs=(anywhere,) * 3,
-        scratch_shapes=[dma((3,))],
+        scratch_shapes=[vmem((5, PLANES, ROWS, COLS), f32), dma((5,))],
     )(*(pltpu.with_memory_space_constraint(x, pltpu.VMEM) for x in results))
 
 

time: 31.7 us -> 31 us (0.978)
  Pallas kernels: 30.9 us -> 30.3 us
    pallas_call x2, Pallas kernels: 30.9 us -> 30.3 us  [the longest x1 29.4 us: local(): pl.pallas_call(body, out_shape=shapes + (jax.ShapeDtypeStruct((5, ROWS, C...]
where the time goes in v7:
time: 31 us; the launch traced here: 30.9 us
  Pallas kernels  30.3 us (98%)
  between operations  0.64 us (2%)
    pallas_call x1, Pallas kernels, local(): pl.pallas_call(body, out_shape=shapes + (jax.ShapeDtypeStruct((5, ROWS, C...  29.4 us
    pallas_call x1, Pallas kernels, local(): pl.pallas_call(hand_over, out_shape=shapes, in_specs=[inside] * 4, out_sp...  0.91 us

profile of v7, /device:TPU:1, one launch (start us, length us, event | category | flops | bytes accessed | tf_op | source)
XLA Modules:
  0.0 30.9 jit_solution(5230013338444266661)
XLA Ops:
  0.6 29.4 %shard_map.112 = (f32[1,6,32,128]{3,2,1,0:T(8,128)S(1)}, f32[1,3,6,32,128]{4,3,2,1,0:T(8,128)S(1)}, f32[1,6,32,128]{3,2,1,0:T(8,128)S(1)}, f32[5,32,128]{2,1,0:T(8,128)S(1)}) custom-call(s32[32]{0:T(128)} %placed_hbm.1, s32[2,32]{1,0:T(2,128)} %bitcast.3, s32[2,32]{1,0:T(2,128)} %bitcast.4, s32[2,32]{1,0:T(2,128)} %bitcast.5, f32[1,6,32,128]{3,2,1,0:T(8,128)} %dens_hbm.1, ...), custom_call_target="tpu_custom_call" | custom-call | tf_op jit(solution)/shard_map/pallas_call | solution.py:655
  30.0 0.9 %shard_map.113 = (f32[1,6,32,128]{3,2,1,0:T(8,128)}, f32[1,3,6,32,128]{4,3,2,1,0:T(8,128)}, f32[1,6,32,128]{3,2,1,0:T(8,128)}) custom-call(f32[1,6,32,128]{3,2,1,0:T(8,128)S(1)} %get-tuple-element.7.d, f32[1,3,6,32,128]{4,3,2,1,0:T(8,128)S(1)} %get-tuple-element.8.m, f32[1,6,32,128]{3,2,1,0:T(8,128)S(1)} %get-tuple-element.9.e, ...), custom_call_target="tpu_custom_call" | custom-call | tf_op jit(solution)/shard_map/pallas_call | solution.py:702

commit v8 on v7

--- a/solution.py
+++ b/solution.py
@@ -201,7 +201,7 @@
     keep[0], keep[1] = iv, rw
 
 
-def section_ends(ghost, held_ends, lf, lines1, keep, dt):
+def section_ends(ghost, held_ends, lf, dt):
     few = slice(0, 4)
     ga, gb, gd = ghost[72:76, :], ghost[76:80, :], ghost[80:84, :]
     theirs = apart(ga, gb)
@@ -211,8 +211,6 @@
     for n, f in enumerate(flux(*ends[:4], prim, hax, hay) + prim[5]):
         lf[n, LOW, :] = f[0:2]
         lf[n, HIGH, :] = f[2:4]
-    for ch in range(5):
-        lines1[ch] = lines1[ch] + row_rate(lf, keep[0], keep[1], ch)
     return edge_terms(
         [held_ends[7 + n, few, :] for n in range(9)],
         edge_values(theirs, *(spread(shift_lanes(gb, -n)) for n in (112, 120)), dt),
@@ -340,59 +338,76 @@
             metric_ends[n, at, :] = metric_line(x)
 
 
-def line_result(lines1, inner, inner_ends, metric, metric_ends, terms, lf, last, at_start, at_end, before, dt):
-    shape = (ROWS, COLS)
+def line_result(
+    lines2, gb, inner, inner_ends, metric, metric_ends, terms, lf, last, at_start, at_end, before, dt, store, finish
+):
+    shape = (CHUNK, COLS)
     t, left = lanes(shape) & 7, lanes(shape) < 64
     near = t < 4
 
     def join(p, own):
         return jnp.where(left, jnp.where(near, shift_lanes(p, -2), own), jnp.where(near, own, shift_lanes(p, 2)))
 
-    fields = [join(lines1[ch], inner[ch]) for ch in range(5)]
-    gbx, gby = join(lines1[5], metric[2]), join(lines1[6], metric[3])
-    gax, gay, inv, rw, cw = (metric[n] for n in (0, 1, 4, 5, 6))
-    prim = primitives(*fields, dt)
-    curved = prim[5]
-    for n, f in enumerate(flux(*fields[:4], prim, gax, gay) + curved):
-        lf[n, CHUNK : CHUNK + ROWS, :] = f
-    few = slice(0, 4)
-    te, le = lanes((4, COLS)) & 7, lanes((4, COLS)) < 64
-
-    def place(e):
-        here = jnp.where(le & ((te >> 1) == 1), shift_lanes(e, -2), 0.0)
-        return jnp.where(jnp.logical_not(le) & ((te >> 1) == 2), shift_lanes(e, 66), here)
-
-    inv_e, cw_e = metric_ends[2, few, :], metric_ends[3, few, :]
-    ends = []
-    for ch in range(5):
-        h = inner_ends[ch, few, :] - place(terms[ch]) * ((before / 12.0) * inv_e)
-        if ch > 0:
-            h = h + cw_e * place(terms[4 + ch])
-        sign = -1.0 if 1 <= ch <= 3 else 1.0
-        f = fields[ch]
-        wall = jnp.concatenate([sign * f[1:2], sign * f[0:1], f[31:32], f[30:31]], axis=0)
-        r = rows_of((4, COLS))
-        use = jnp.where(at_start, 1, 0) * jnp.where(r < 2, 1, 0) + jnp.where(at_end, 1, 0) * jnp.where(r >= 2, 1, 0)
-        ends.append(jnp.where(use > 0, wall, h))
-    end_prim = primitives(*ends, dt)
-    for n, f in enumerate(
-        flux(*ends[:4], end_prim, metric_ends[0, few, :], metric_ends[1, few, :]) + end_prim[5]
-    ):
-        lf[n, LOW, :] = f[0:2]
-        lf[n, HIGH, :] = f[2:4]
-    iv = (dt / 12.0) * inv
-    center = -30.0 * (rw + cw + 1.0)
-    fj = flux(*fields[:4], prim, gbx, gby)
-    fk = flux_planes(*fields[1:4], prim)
-    for ch in range(5):
-        value = 0.5 * fields[ch] + row_rate(lf, iv, rw, ch) + cross_rate(fj, fk, curved, iv, cw, center, ch, dt)
-        last[ch] = jnp.where((t >= 2) & (t < 6), value, shift_lanes(value, -68))
-
-
-def row_rate(lf, iv, rw, ch):
-    value = -(slope(*(lf[ch, CHUNK + d : CHUNK + d + ROWS, :] for d in (-2, -1, 1, 2))) * iv)
+    kept = {}
+    for c in store:
+        rows = slice(c * CHUNK, (c + 1) * CHUNK)
+        fields = [join(lines2[ch, rows, :], inner[ch, rows, :]) for ch in range(5)]
+        prim = primitives(*fields, dt)
+        for n, f in enumerate(flux(*fields[:4], prim, metric[0, rows, :], metric[1, rows, :]) + prim[5]):
+            lf[n, span(c), :] = f
+        kept[c] = (rows, fields, prim)
+    if terms is not None:
+        few = slice(0, 4)
+        te, le = lanes((4, COLS)) & 7, lanes((4, COLS)) < 64
+
+        def place(e):
+            here = jnp.where(le & ((te >> 1) == 1), shift_lanes(e, -2), 0.0)
+            return jnp.where(jnp.logical_not(le) & ((te >> 1) == 2), shift_lanes(e, 66), here)
+
+        inv_e, cw_e = metric_ends[2, few, :], metric_ends[3, few, :]
+        ends = []
+        for ch in range(5):
+            h = inner_ends[ch, few, :] - place(terms[ch]) * ((before / 12.0) * inv_e)
+            if ch > 0:
+                h = h + cw_e * place(terms[4 + ch])
+            sign = -1.0 if 1 <= ch <= 3 else 1.0
+            f, g = kept[0][1][ch], kept[3][1][ch]
+            wall = jnp.concatenate([sign * f[1:2], sign * f[0:1], g[7:8], g[6:7]], axis=0)
+            r = rows_of((4, COLS))
+            use = jnp.where(at_start, 1, 0) * jnp.where(r < 2, 1, 0) + jnp.where(at_end, 1, 0) * jnp.where(r >= 2, 1, 0)
+            ends.append(jnp.where(use > 0, wall, h))
+        end_prim = primitives(*ends, dt)
+        for n, f in enumerate(
+            flux(*ends[:4], end_prim, metric_ends[0, few, :], metric_ends[1, few, :]) + end_prim[5]
+        ):
+            lf[n, LOW, :] = f[0:2]
+            lf[n, HIGH, :] = f[2:4]
+    for c in finish:
+        rows, fields, prim = kept[c]
+        gbx, gby = (join(gb[5 + n, rows, :], metric[2 + n, rows, :]) for n in range(2))
+        inv, rw, cw = (metric[n, rows, :] for n in (4, 5, 6))
+        iv = (dt / 12.0) * inv
+        center = -30.0 * (rw + cw + 1.0)
+        fj = flux(*fields[:4], prim, gbx, gby)
+        fk = flux_planes(*fields[1:4], prim)
+        for ch in range(5):
+            value = 0.5 * fields[ch] + row_rate(lf, iv, rw, ch, rows)
+            value = value + cross_rate(fj, fk, prim[5], iv, cw, center, ch, dt)
+            last[ch, rows, :] = jnp.where((t >= 2) & (t < 6), value, shift_lanes(value, -68))
+
+
+def add_rows(lf, lines1, lines2, keep, chunks):
+    for c in chunks:
+        rows = slice(c * CHUNK, (c + 1) * CHUNK)
+        for ch in range(5):
+            lines2[ch, rows, :] = lines1[ch, rows, :] + row_rate(lf, keep[0, rows, :], keep[1, rows, :], ch, rows)
+
+
+def row_rate(lf, iv, rw, ch, rows):
+    base, size = CHUNK + rows.start, rows.stop - rows.start
+    value = -(slope(*(lf[ch, base + d : base + d + size, :] for d in (-2, -1, 1, 2))) * iv)
     if ch > 0:
-        value = value + rw * curve(*(lf[4 + ch, CHUNK + d : CHUNK + d + ROWS, :] for d in (-2, -1, 1, 2)))
+        value = value + rw * curve(*(lf[4 + ch, base + d : base + d + size, :] for d in (-2, -1, 1, 2)))
     return value
 
 
@@ -456,7 +471,7 @@
     placed_hbm, neighbour_hbm, face_hbm, orient_hbm, dens_hbm, mom_hbm, ener_hbm, met_hbm, vol_hbm,
     out_d, out_m, out_e, last,
     placed, neighbour, face, orient, load,
-    ex, exm, sec, fi, wi, part, lf, lf2, lines1, inner, inner_ends, metric, metric_ends,
+    ex, exm, sec, fi, wi, part, lf, lf2, lines1, lines2, inner, inner_ends, metric, metric_ends,
     held, held_ends, keep,
     strips, relay, arrived, got, both, picked, got2, both_e, picked_e, got2_e, ghost,
     send1, recv1, send_h, recv_h, send2, recv2, send_f, recv_f, send_e, recv_e, send_r, recv_r, send_m, recv_m,
@@ -618,12 +633,19 @@
         copy.wait_recv()
     ghost[0:72, :] = settle(jnp.where(near, got2[origin[0]], got2[origin[1]]), main_sign, table)
     section_main(ghost, held, lf, lines1, keep, time_step)
+    add_rows(lf, lines1, lines2, keep, range(4))
+    line_result(
+        lines2, lines1, inner, inner_ends, metric, metric_ends, None, lf2, last,
+        at_start, at_end, time_step, half, range(4), (1, 2),
+    )
     for copy in hop2[7:]:
         copy.wait_recv()
     ghost[72:88, :] = settle(jnp.where(near[:16], got2_e[origin[0]], got2_e[origin[1]]), ends_sign, table)
-    terms = section_ends(ghost, held_ends, lf, lines1, keep, time_step)
+    terms = section_ends(ghost, held_ends, lf, time_step)
+    add_rows(lf, lines1, lines2, keep, (0, 3))
     line_result(
-        lines1, inner, inner_ends, metric, metric_ends, terms, lf2, last, at_start, at_end, time_step, half
+        lines2, lines1, inner, inner_ends, metric, metric_ends, terms, lf2, last,
+        at_start, at_end, time_step, half, (0, 3), (0, 3),
     )
     for copy in list(hop1.values()) + list(hop_ends.values()) + hop2:
         copy.wait_send()
@@ -669,6 +691,7 @@
             vmem((9, padded, COLS), f32),
             vmem((9, padded, COLS), f32),
             vmem((7, ROWS, COLS), f32),
+            vmem((5, ROWS, COLS), f32),
             vmem((5, ROWS, COLS), f32),
             vmem((5, CHUNK, COLS), f32),
             vmem((7, ROWS, COLS), f32),

time: 31 us -> 32 us (1.032)
  Pallas kernels: 30.3 us -> 31.2 us
    pallas_call x1, Pallas kernels: 29.4 us -> 30.3 us  [local(): pl.pallas_call(body, out_shape=shapes + (jax.ShapeDtypeStruct((5, ROWS, C...]
where the time goes in v8:
time: 32 us; the launch traced here: 31.9 us
  Pallas kernels  31.2 us (98%)
  between operations  0.64 us (2%)
    pallas_call x1, Pallas kernels, local(): pl.pallas_call(body, out_shape=shapes + (jax.ShapeDtypeStruct((5, ROWS, C...  30.3 us
    pallas_call x1, Pallas kernels, local(): pl.pallas_call(hand_over, out_shape=shapes, in_specs=[inside] * 4, out_sp...  0.91 us

profile of v8, /device:TPU:1, one launch (start us, length us, event | category | flops | bytes accessed | tf_op | source)
XLA Modules:
  0.0 31.9 jit_solution(4355841182329623117)
XLA Ops:
  0.6 30.3 %shard_map.112 = (f32[1,6,32,128]{3,2,1,0:T(8,128)S(1)}, f32[1,3,6,32,128]{4,3,2,1,0:T(8,128)S(1)}, f32[1,6,32,128]{3,2,1,0:T(8,128)S(1)}, f32[5,32,128]{2,1,0:T(8,128)S(1)}) custom-call(s32[32]{0:T(128)} %placed_hbm.1, s32[2,32]{1,0:T(2,128)} %bitcast.3, s32[2,32]{1,0:T(2,128)} %bitcast.4, s32[2,32]{1,0:T(2,128)} %bitcast.5, f32[1,6,32,128]{3,2,1,0:T(8,128)} %dens_hbm.1, ...), custom_call_target="tpu_custom_call" | custom-call | tf_op jit(solution)/shard_map/pallas_call | solution.py:677
  31.0 0.9 %shard_map.113 = (f32[1,6,32,128]{3,2,1,0:T(8,128)}, f32[1,3,6,32,128]{4,3,2,1,0:T(8,128)}, f32[1,6,32,128]{3,2,1,0:T(8,128)}) custom-call(f32[1,6,32,128]{3,2,1,0:T(8,128)S(1)} %get-tuple-element.7.d, f32[1,3,6,32,128]{4,3,2,1,0:T(8,128)S(1)} %get-tuple-element.8.m, f32[1,6,32,128]{3,2,1,0:T(8,128)S(1)} %get-tuple-element.9.e, ...), custom_call_target="tpu_custom_call" | custom-call | tf_op jit(solution)/shard_map/pallas_call | solution.py:725
